TPU v7x, 512 devices: a whole 4x8x8 slice. The times are simulated.
512 devices in a mesh: fsdp: 16 (over x, z_lo), space: 32 (over y, z_hi, core).
Axes of the slice: x: 4, y: 8, z: 8 (z_hi: 2, z_lo: 4; z = z_hi * 4 + z_lo), core: 2. Of those that a mesh axis runs over, the one named last changes fastest.
Arguments:
- images: bfloat16 [16, 768, 128, 256], P('fsdp', 'space'), may hold values from -6 to 6
- kernel: bfloat16 [256, 3, 3, 256], P('fsdp'), may hold values from -0.125 to 0.125
- cotangent: bfloat16 [16, 384, 64, 256], P('fsdp', 'space'), may hold values from -6 to 6
Outputs:
- output: bfloat16 [16, 384, 64, 256], P('fsdp', 'space')
- grad_input: bfloat16 [16, 768, 128, 256], P('fsdp', 'space')
- grad_kernel: float32 [256, 3, 3, 256], P('fsdp', None, None, 'space')
- penalty_rows: float32 [256], P('fsdp')
All inputs are finite; a program needn't handle non-finite values.
Results may differ from a plain program's by a relative error of at most 0.0034.
Values may be sent and summed in bfloat16 or wider, within the bound.
No kernel may reach another device: no remote copies, remote signals or barrier semaphores. Data moves between devices by JAX's collectives and lax.ppermute only.
A program may use at most 64 MiB of HBM per device.

v0:
```python
import jax
import jax.numpy as jnp
from jax import lax
from jax.sharding import PartitionSpec as P

PEN_WEIGHT = 4.0


def shifted_2(block, axis, distance):
    devices = range(lax.axis_size(axis))
    route = [(i - distance, i) for i in devices if i - distance in devices]
    return lax.ppermute(block, axis, route)


def shifted(padded, row_shift, col_shift):
    return padded[:, 2 + row_shift : 5 + row_shift, 2 + col_shift : 5 + col_shift, :]


def penalty_terms(own_panel, gathered, first_row, offset, slice_width):
    own_count = own_panel.shape[0]
    channels = gathered.shape[0]
    spread = ((0, 0), (2, 2), (2, 2), (0, 0))
    own_pad = jnp.pad(own_panel, spread)
    share = lax.dynamic_slice_in_dim(gathered, offset, slice_width, 3)
    share_pad = jnp.pad(share, spread)
    whole_flat = gathered.reshape(channels, -1)
    identity_rows = (
        lax.broadcasted_iota(jnp.int32, (own_count, channels), 0) + first_row
        == lax.broadcasted_iota(jnp.int32, (own_count, channels), 1)
    ).astype(jnp.float32)
    row_penalty = jnp.zeros((own_count,), jnp.float32)
    pen_grad = jnp.zeros((own_count, 9 * slice_width), jnp.float32)
    for row_shift in (-2, 0, 2):
        for col_shift in (-2, 0, 2):
            moved_rows = shifted(own_pad, row_shift, col_shift).reshape(own_count, -1)
            gram_block = lax.dot_general(
                moved_rows, whole_flat, (((1,), (1,)), ((), ())), preferred_element_type=jnp.float32
            )
            if row_shift == 0 and col_shift == 0:
                gram_block = gram_block - identity_rows
            row_penalty = row_penalty + jnp.sum(gram_block * gram_block, axis=1)
            back_flat = (
                shifted(share_pad, -row_shift, -col_shift).reshape(channels, -1).astype(jnp.float32)
            )
            pen_grad = pen_grad + jnp.dot(gram_block, back_flat, precision=lax.Precision.HIGHEST)
    return (row_penalty, 4.0 * pen_grad.reshape(own_count, 3, 3, slice_width))


def gather_patches(padded, out_rows, out_cols):
    pieces = [
        padded[:, tap_row : tap_row + 2 * out_rows : 2, tap_col : tap_col + 2 * out_cols : 2, :]
        for tap_row in range(3)
        for tap_col in range(3)
    ]
    joined = jnp.concatenate(pieces, axis=-1)
    return joined.reshape(-1, joined.shape[-1])


def fold_taps(tap_sums):
    strip_count, grid_rows, grid_cols = tap_sums.shape[:3]
    channels = tap_sums.shape[-1]
    row_pad = ((0, 0), (0, 1), (0, 0), (0, 0), (0, 0))
    even_rows = jnp.pad(tap_sums[:, :, :, 0], row_pad) + jnp.pad(
        tap_sums[:, :, :, 2], ((0, 0), (1, 0), (0, 0), (0, 0), (0, 0))
    )
    odd_rows = jnp.pad(tap_sums[:, :, :, 1], row_pad)
    merged = jnp.stack([even_rows, odd_rows], axis=2).reshape(
        strip_count, 2 * grid_rows + 2, grid_cols, 3, channels
    )[:, : 2 * grid_rows + 1]
    col_pad = ((0, 0), (0, 0), (0, 1), (0, 0))
    even_cols = jnp.pad(merged[:, :, :, 0], col_pad) + jnp.pad(
        merged[:, :, :, 2], ((0, 0), (0, 0), (1, 0), (0, 0))
    )
    odd_cols = jnp.pad(merged[:, :, :, 1], col_pad)
    total_rows = merged.shape[1]
    return jnp.stack([even_cols, odd_cols], axis=3).reshape(
        strip_count, total_rows, 2 * grid_cols + 2, channels
    )[:, :, : 2 * grid_cols + 1]


def per_device(images, kernel, cotangent):
    strip_count, row_count, col_count, channels = images.shape
    out_rows = row_count // 2
    out_cols = col_count // 2
    panel_size = kernel.shape[0]
    gathered = lax.all_gather(kernel, "fsdp", axis=0, tiled=True)
    out_channels = gathered.shape[0]
    whole_flat = gathered.reshape(out_channels, 9 * channels)
    upper_row = shifted_2(images[:, row_count - 1 :], "space", 1)
    padded = jnp.concatenate([upper_row, images], axis=1)
    padded = jnp.pad(padded, ((0, 0), (0, 0), (1, 0), (0, 0)))
    patches = gather_patches(padded, out_rows, out_cols)
    product = lax.dot_general(
        patches, whole_flat, (((1,), (1,)), ((), ())), preferred_element_type=jnp.float32
    )
    output = product.astype(jnp.bfloat16).reshape(strip_count, out_rows, out_cols, out_channels)
    lower_row = shifted_2(cotangent[:, :1], "space", -1)
    extended = jnp.concatenate([cotangent, lower_row], axis=1)
    tap_sums = jnp.dot(
        extended.reshape(-1, out_channels), whole_flat, preferred_element_type=jnp.float32
    )
    tap_sums = tap_sums.reshape(strip_count, out_rows + 1, out_cols, 3, 3, channels)
    folded = fold_taps(tap_sums)
    grad_input = folded[:, 1 : row_count + 1, 1 : col_count + 1].astype(jnp.bfloat16)
    cot_flat = cotangent.reshape(-1, out_channels)
    own_rows = lax.psum_scatter(
        lax.dot_general(
            cot_flat, patches, (((0,), (0,)), ((), ())), preferred_element_type=jnp.float32
        ),
        "fsdp",
        scatter_dimension=0,
        tiled=True,
    )
    own_grad = lax.psum_scatter(
        own_rows.reshape(panel_size, 3, 3, channels), "space", scatter_dimension=3, tiled=True
    )
    first_row = lax.axis_index("fsdp") * panel_size
    slice_width = channels // lax.axis_size("space")
    offset = lax.axis_index("space") * slice_width
    row_penalty, pen_grad = penalty_terms(kernel, gathered, first_row, offset, slice_width)
    strip_rows = out_rows * lax.axis_size("space")
    grad_kernel = own_grad / strip_rows + PEN_WEIGHT * pen_grad
    return (output, grad_input, grad_kernel, row_penalty)


def solution(mesh):
    in_specs = (
        P("fsdp", "space", None, None),
        P("fsdp", None, None, None),
        P("fsdp", "space", None, None),
    )
    out_specs = (
        P("fsdp", "space", None, None),
        P("fsdp", "space", None, None),
        P("fsdp", None, None, "space"),
        P("fsdp"),
    )
    return jax.shard_map(
        per_device, mesh=mesh, in_specs=in_specs, out_specs=out_specs, check_vma=False
    )
```

profile of v0, /device:TPU:6, one launch (start us, length us, event | category | flops | bytes accessed | tf_op | source)
XLA Modules:
  0.0 334.3 jit_solution(3470023973481236146)
XLA Ops:
  8.7 1.3 collective-permute-start.1
  10.8 3.0 collective-permute-start
  14.8 2.2 fusion.3
  19.2 3.9 %slice.117 = bf16[1,12,64,256]{3,2,1,0:T(8,128)(2,1)} slice(bf16[1,25,129,256]{3,2,1,0:T(8,128)(2,1)S(1)} %fusion.3), slice={[0:1:1], [1:25:2], [1:129:2], [0:256:1]} | slice | bytes 786432 | tf_op jit(solution)/shard_map/slice | solution.py:51
  23.1 3.9 %slice.116 = bf16[1,12,64,256]{3,2,1,0:T(8,128)(2,1)} slice(bf16[1,25,129,256]{3,2,1,0:T(8,128)(2,1)S(1)} %fusion.3), slice={[0:1:1], [1:25:2], [0:128:2], [0:256:1]} | slice | bytes 786432 | tf_op jit(solution)/shard_map/slice | solution.py:51
  27.0 4.0 %slice.115 = bf16[1,12,64,256]{3,2,1,0:T(8,128)(2,1)} slice(bf16[1,25,129,256]{3,2,1,0:T(8,128)(2,1)S(1)} %fusion.3), slice={[0:1:1], [0:24:2], [2:129:2], [0:256:1]} | slice | bytes 786432 | tf_op jit(solution)/shard_map/slice | solution.py:51
  31.1 4.0 %slice.114 = bf16[1,12,64,256]{3,2,1,0:T(8,128)(2,1)} slice(bf16[1,25,129,256]{3,2,1,0:T(8,128)(2,1)S(1)} %fusion.3), slice={[0:1:1], [0:24:2], [1:129:2], [0:256:1]} | slice | bytes 786432 | tf_op jit(solution)/shard_map/slice | solution.py:51
  35.0 4.0 %slice.113 = bf16[1,12,64,256]{3,2,1,0:T(8,128)(2,1)} slice(bf16[1,25,129,256]{3,2,1,0:T(8,128)(2,1)S(1)} %fusion.3), slice={[0:1:1], [0:24:2], [0:128:2], [0:256:1]} | slice | bytes 786432 | tf_op jit(solution)/shard_map/slice | solution.py:51
  40.1 1.1 constant_dynamic-update-slice_fusion.8
  41.2 1.0 constant_dynamic-update-slice_fusion.7
  42.2 1.0 constant_dynamic-update-slice_fusion.6
  43.5 1.7 copy-done.6
  45.2 1.1 convolution_bitcast_fusion
  46.4 2.0 copy.68
  48.4 45.2 %all-gather.2.cloned.1.call-done = bf16[256,3,3,256]{3,0,2,1:T(8,128)(2,1)} async-done(((bf16[16,3,3,256]{3,0,2,1:T(8,128)(2,1)}), bf16[256,3,3,256]{3,0,2,1:T(8,128)(2,1)}) %all-gather.2.cloned.1.call-update) | async-done | bytes 1179664 | tf_op jit(solution)/shard_map/all_gather | solution.py:86
  93.7 1.3 constant_dynamic-slice_fusion
  95.0 2.6 pad_slice_fusion
  97.6 1.2 copy.49
  98.8 1.3 copy.48
  104.6 1.3 copy.56
  105.9 1.3 copy.50
  107.2 1.3 copy.51
  108.4 1.3 copy.53
  113.5 1.2 convolution_bitcast_fusion.1
  118.9 1.4 copy.47
  120.3 3.5 %reshape.88 = bf16[1,27,130,256]{3,2,1,0:T(8,128)(2,1)} reshape(bf16[1,27,65,2,256]{4,3,2,1,0:T(2,128)(2,1)S(1)} %copy.47) | data formatting | bytes 3594240 | tf_op jit(solution)/shard_map/reshape | solution.py:76
  123.8 3.2 slice.152
  127.0 3.8 %convolution_convert_fusion = bf16[768,256]{1,0:T(8,128)(2,1)} fusion(bf16[768,2304]{1,0:T(8,128)(2,1)} %bitcast.159, bf16[256,2304]{0,1:T(8,128)(2,1)S(1)} %bitcast.147), kind=kOutput, calls=%fused_computation.26 | convolution fusion | flops 906166272 | bytes 5111808 | tf_op jit(solution)/shard_map/dot_general | solution.py:93
  130.9 60.9 %reduce-scatter.7.cloned.1.call-done = f32[16,2304]{1,0:T(8,128)} async-done(((f32[256,2304]{1,0:T(8,128)}), f32[16,2304]{1,0:T(8,128)}) %reduce-scatter.7.cloned.1.call-update) | async-done | bytes 147472
  191.7 2.3 copy.69
  194.6 131.8 %reduce-scatter.5.cloned.1.call-done = f32[16,3,3,8]{0,3,2,1:T(8,128)} async-done(((f32[16,3,3,256]{0,3,2,1:T(8,128)}), f32[16,3,3,8]{0,3,2,1:T(8,128)}) %reduce-scatter.5.cloned.1.call-update) | async-done | bytes 4624 | tf_op jit(solution)/shard_map/reduce_scatter | solution.py:114
  326.3 1.4 multiply_add_fusion
  (67 shorter events, 19.6 us)
Async XLA Ops:
  7.2 86.5 %all-gather.2.cloned.1.call-start = ((), (), s32[]{:S(2)}) async-start(), calls=%async_computation.2 | async-start | bytes 1253376 | tf_op jit(solution)/shard_map/all_gather | solution.py:86
  7.9 183.8 %reduce-scatter.7.cloned.1.call-start = ((), (), s32[]{:S(2)}) async-start(), calls=%async_computation.4 | async-start | bytes 2506752
  8.7 104.7 %collective-permute-start.1 = (bf16[1,1,64,256]{3,2,1,0:T(8,128)(2,1)S(1)}, bf16[1,1,64,256]{3,2,1,0:T(8,128)(2,1)S(1)}, u32[]{:S(2)}, u32[]{:S(2)}) collective-permute-start(bf16[1,1,64,256]{3,2,1,0:T(8,128)(2,1)S(1)} %slice.122), channel_id=1, source_target_pairs={{1,0},{2,1},{3,2},{4,3},{5,4},{6,5},{7,6},{8,7},{9,8},{10,9},{11,1... | collective-permute-start | bytes 98312 | tf_op jit(solution)/shard_map/ppermute | solution.py:12
  10.8 3.9 %collective-permute-start = (bf16[1,1,128,256]{3,2,1,0:T(8,128)(2,1)S(1)}, bf16[1,1,128,256]{3,2,1,0:T(8,128)(2,1)S(1)}, u32[]{:S(2)}, u32[]{:S(2)}) collective-permute-start(bf16[1,1,128,256]{3,2,1,0:T(8,128)(2,1)S(1)} %slice.112), channel_id=1, source_target_pairs={{0,1},{1,2},{2,3},{3,4},{4,5},{5,6},{6,7},{7,8},{8,9},{9,10},{10,1... | collective-permute-start | bytes 196616 | tf_op jit(solution)/shard_map/ppermute | solution.py:12
  40.1 3.2 copy-start.3
  40.1 3.2 copy-start.2
  43.2 2.0 copy-start.4
  43.5 1.8 copy-start.6
  48.4 277.9 %reduce-scatter.5.cloned.1.call-start = ((), (), s32[]{:S(2)}) async-start(), calls=%async_computation.3 | async-start | bytes 1216512 | tf_op jit(solution)/shard_map/reduce_scatter | solution.py:114
  95.0 5.1 %copy-start = (bf16[256,3,3,256]{3,0,2,1:T(8,128)(2,1)S(1)}, bf16[256,3,3,256]{3,0,2,1:T(8,128)(2,1)}, u32[]{:S(2)}) copy-start(bf16[256,3,3,256]{3,0,2,1:T(8,128)(2,1)} %all-gather.2.cloned.1.call-done) | copy-start | bytes 3538948
  95.0 5.1 %copy-start.1 = (bf16[16,3,3,256]{3,0,2,1:T(8,128)(2,1)S(1)}, bf16[16,3,3,256]{3,0,2,1:T(8,128)(2,1)}, u32[]{:S(2)}) copy-start(bf16[16,3,3,256]{3,0,2,1:T(8,128)(2,1)} %param.4) | copy-start | bytes 221188
  110.2 3.3 copy-start.5
Sparse Core Ops, SparseCore 0:
  10.1 83.5 all-gather.1
  96.5 95.1 reduce-scatter.6
  196.4 129.8 reduce-scatter.4
where the time goes:
time: 335 us; the launch traced here: 334 us
  waiting for transfers between devices  239 us (71%)
  local copies, waits for them, and re-layouts  57.5 us (17%)
  between operations  14.1 us (4%)
  matrix products  12.7 us (4%)
  other arithmetic  6.11 us (2%)
  starting transfers between devices  4.42 us (1%)
    reduce_scatter x1, waiting for transfers between devices, per_device(): lax.psum_scatter(own_rows.reshape(panel_size, 3, 3, channels), 'space', s...  132 us
    unnamed x4, waiting for transfers between devices  61.6 us
    all_gather x1, waiting for transfers between devices, per_device(): gathered = lax.all_gather(kernel, 'fsdp', axis=0, tiled=True)  45.2 us
    slice x9, local copies, waits for them, and re-layouts, gather_patches(): padded[:, tap_row:tap_row + 2 * out_rows:2, tap_col:tap_col + 2 * out_col...  23 us
    slice x9, local copies, waits for them, and re-layouts, shifted(): padded[:, 2 + row_shift:5 + row_shift, 2 + col_shift:5 + col_shift, :]  10.6 us
    unnamed x24, local copies, waits for them, and re-layouts  9.34 us
  transfers between devices with their start and end apart: 5, of which 4 were waited for; matrix products, arithmetic and copies ran while one was open for 21% of the time, Pallas kernels for 0%

commit v1 on v0

v1 whole, which is shorter than its diff:
```python
import jax
import jax.numpy as jnp
from jax import lax
from jax.experimental import pallas as pl
from jax.experimental.pallas import tpu as pltpu
from jax.sharding import Mesh, PartitionSpec as P

PEN_WEIGHT = 4.0
BF = jnp.bfloat16
F32 = jnp.float32

ROWS, COLS, CH = 24, 128, 256
R, Q = 12, 64
POS = R * Q
TAPS = [(i, j) for i in range(3) for j in range(3)]
SHIFTS = [(u, v) for u in (-2, 0, 2) for v in (-2, 0, 2)]

NT = (((1,), (1,)), ((), ()))


def mm(a, b):
    return jnp.dot(a, b, preferred_element_type=F32)


def mm_nt(a, b):
    return lax.dot_general(a, b, NT, preferred_element_type=F32)


def one_hot(cond):
    return jnp.where(cond, 1.0, 0.0).astype(BF)


def iota2(shape, axis):
    return lax.broadcasted_iota(jnp.int32, shape, axis)


def column_sorter():
    row, col = iota2((COLS, COLS), 0), iota2((COLS, COLS), 1)
    return one_hot(col == 2 * (row % Q) + row // Q)


def shift_left(block):
    moved = pltpu.roll(block, Q - 1, 0)
    return jnp.where(iota2(block.shape, 0) == Q - 1, 0.0, moved)


def shift_right(block):
    moved = pltpu.roll(block, 1, 0)
    return jnp.where(iota2(block.shape, 0) == 0, 0.0, moved)


def wgrad_kernel(
    core_ref, img_ref, cot_ref, low_ref,
    keep_ref, send_ref, ee_ref, eo_ref, oe_ref, oo_ref, cot_s_ref,
    per_ref, cot_t_ref,
):
    core = core_ref[0]
    sorter = column_sorter()
    chan, slot = iota2((CH, CH), 0), iota2((CH, CH), 1)
    other = jnp.where((chan // 8) % 2 == core, 0, 1)
    to_core = one_hot(slot == (chan // 16) * 8 + chan % 8 + (CH // 2) * other)
    for r in range(R):
        for parity, (even_ref, odd_ref) in enumerate(((ee_ref, eo_ref), (oe_ref, oo_ref))):
            split = mm(sorter, img_ref[2 * r + parity]).astype(BF)
            even_ref[r * Q : (r + 1) * Q] = split[:Q]
            odd_ref[r * Q : (r + 1) * Q] = split[Q:]
    for k, ref in enumerate((ee_ref, eo_ref, oe_ref, oo_ref)):
        per_ref[k] = mm(ref[...], to_core).astype(BF)
    for r in range(R + 1):
        row = cot_ref[r] if r < R else low_ref[...]
        cot_s_ref[r * Q : (r + 1) * Q] = shift_left(row.astype(F32)).astype(BF)
    cot = cot_ref[...].reshape(POS, CH)
    below = jnp.concatenate([cot[Q:], low_ref[...]], axis=0)
    cot_t_ref[0] = cot.T
    cot_t_ref[1] = below.T
    cot_t_ref[2] = cot_s_ref[0:POS].T
    cot_t_ref[3] = cot_s_ref[Q : Q + POS].T
    for t, (i, j) in enumerate(TAPS):
        grad_rows = (1 if i == 0 else 0) + (2 if j == 0 else 0)
        image = (0 if i == 1 else 2) + (0 if j == 1 else 1)
        tap = mm(cot_t_ref[grad_rows], per_ref[image]).reshape(16, 16, CH)
        keep_ref[:, t] = tap[:, :, : CH // 2]
        send_ref[:, t] = tap[:, :, CH // 2 :].astype(BF)


def conv_kernel(
    place_ref, mine_ref, other_ref, up_ref, low_ref, cot_ref, cot_s_ref,
    ee_ref, eo_ref, oe_ref, oo_ref,
    out_ref, gin_ref, pen_ref, row_ref,
    w_ref, acc_ref, z_ref,
):
    core, x, zl, space = place_ref[0], place_ref[1], place_ref[2], place_ref[3]
    half = CH // 2
    for a, dx in enumerate((0, 1, 3, 2)):
        for b, dz in enumerate((0, 1, 3, 2)):
            first = pl.multiple_of((((x + dx) % 4) * 4 + (zl + dz) % 4) * 16, 16)
            rows = slice((a * 4 + b) * 16, (a * 4 + b + 1) * 16)

            @pl.when(core == 0)
            def _(first=first, rows=rows):
                for t in range(9):
                    lanes = slice(t * half, (t + 1) * half)
                    w_ref[pl.ds(first, 16), t * CH : t * CH + half] = mine_ref[rows, lanes]
                    w_ref[pl.ds(first, 16), t * CH + half : (t + 1) * CH] = other_ref[rows, lanes]

            @pl.when(core == 1)
            def _(first=first, rows=rows):
                for t in range(9):
                    lanes = slice(t * half, (t + 1) * half)
                    w_ref[pl.ds(first, 16), t * CH : t * CH + half] = other_ref[rows, lanes]
                    w_ref[pl.ds(first, 16), t * CH + half : (t + 1) * CH] = mine_ref[rows, lanes]

    def tap(i, j):
        t = 3 * i + j
        return w_ref[:, t * CH : (t + 1) * CH]

    sorter = column_sorter()
    halo = mm(sorter, up_ref[...]).astype(BF)
    oe_up = jnp.concatenate([halo[:Q], oe_ref[0 : POS - Q]], axis=0)
    oo_up = jnp.concatenate([halo[Q:], oo_ref[0 : POS - Q]], axis=0)
    z_ref[...] = mm_nt(eo_ref[...], tap(1, 0))
    z_ref[...] += mm_nt(oo_ref[...], tap(2, 0))
    z_ref[...] += mm_nt(oo_up, tap(0, 0))
    acc_ref[0] = mm_nt(ee_ref[...], tap(1, 1))
    acc_ref[0] += mm_nt(eo_ref[...], tap(1, 2))
    acc_ref[0] += mm_nt(oe_ref[...], tap(2, 1))
    acc_ref[0] += mm_nt(oo_ref[...], tap(2, 2))
    acc_ref[0] += mm_nt(oe_up, tap(0, 1))
    acc_ref[0] += mm_nt(oo_up, tap(0, 2))
    for r in range(R):
        rows = slice(r * Q, (r + 1) * Q)
        out_ref[r] = (acc_ref[0, rows] + shift_right(z_ref[rows])).astype(BF)
    cot = cot_ref[...].reshape(POS, CH)
    below = jnp.concatenate([cot[Q:], low_ref[...]], axis=0)
    cot_s = cot_s_ref[0:POS]
    below_s = cot_s_ref[Q : Q + POS]
    acc_ref[0] = mm(cot, tap(1, 1))
    acc_ref[1] = mm(cot, tap(1, 2))
    acc_ref[1] += mm(cot_s, tap(1, 0))
    acc_ref[2] = mm(cot, tap(2, 1))
    acc_ref[2] += mm(below, tap(0, 1))
    acc_ref[3] = mm(cot, tap(2, 2))
    acc_ref[3] += mm(cot_s, tap(2, 0))
    acc_ref[3] += mm(below, tap(0, 2))
    acc_ref[3] += mm(below_s, tap(0, 0))
    row, col = iota2((COLS, COLS), 0), iota2((COLS, COLS), 1)
    weaver = one_hot(col == (row % 2) * Q + row // 2)
    for r in range(R):
        rows = slice(r * Q, (r + 1) * Q)
        for parity in range(2):
            both = jnp.concatenate(
                [acc_ref[2 * parity, rows].astype(BF), acc_ref[2 * parity + 1, rows].astype(BF)], axis=0
            )
            gin_ref[2 * r + parity] = mm(weaver, both).astype(BF)
    own_first = pl.multiple_of((x * 4 + zl) * 16, 16)
    own = [w_ref[pl.ds(own_first, 16), t * CH : (t + 1) * CH] for t in range(9)]
    grams = {}
    kin = [[s for s in range(9) if (s // 3 - t // 3) % 2 == 0 and (s % 3 - t % 3) % 2 == 0] for t in range(9)]
    for t in range(9):
        stacked = jnp.concatenate([own[s] for s in kin[t]], axis=0)
        part = mm_nt(stacked, w_ref[:, t * CH : (t + 1) * CH])
        for n, s in enumerate(kin[t]):
            shift = (s // 3 - t // 3, s % 3 - t % 3)
            block = part[n * 16 : (n + 1) * 16]
            grams[shift] = grams[shift] + block if shift in grams else block
    diagonal = iota2((16, CH), 0) + own_first == iota2((16, CH), 1)
    grams[(0, 0)] = grams[(0, 0)] - jnp.where(diagonal, 1.0, 0.0)
    squares = jnp.zeros((16, CH), F32)
    for shift in SHIFTS:
        squares = squares + grams[shift] * grams[shift]
    row_ref[...] = jnp.sum(squares, axis=1, keepdims=True)
    pieces = {}
    for shift in SHIFTS:
        high = grams[shift].astype(BF)
        rest = grams[shift] - high.astype(F32)
        mid = rest.astype(BF)
        pieces[shift] = (high, mid, (rest - mid.astype(F32)).astype(BF))
    grads = [jnp.zeros((16, CH), F32) for _ in range(9)]
    for s in range(9):
        stacked = jnp.concatenate(
            [pieces[(t // 3 - s // 3, t % 3 - s % 3)][p] for t in kin[s] for p in range(3)], axis=0
        )
        part = mm(stacked, w_ref[:, s * CH : (s + 1) * CH])
        for n, t in enumerate(kin[s]):
            for p in range(3):
                grads[t] = grads[t] + part[(3 * n + p) * 16 : (3 * n + p + 1) * 16]
    stacked = jnp.concatenate(grads, axis=0)
    high = stacked.astype(BF)
    rest = stacked - high.astype(F32)
    mid = rest.astype(BF)
    low = (rest - mid.astype(F32)).astype(BF)
    pick = one_hot(iota2((8, CH), 0) + space * 8 == iota2((8, CH), 1))
    pen_ref[...] = mm_nt(pick, high) + mm_nt(pick, mid) + mm_nt(pick, low)


def sum_kernel(parts_ref, out_ref):
    total = parts_ref[0].astype(F32)
    for k in range(1, 4):
        total = total + parts_ref[k].astype(F32)
    turned = total.T
    for k in range(4):
        out_ref[:, k] = turned[:, 144 * k : 144 * (k + 1)].reshape(16, 8, 144).astype(BF)


def call(kernel, name, out_shape, scratch=(), n_scalar=0, n_in=0):
    vmem = pl.BlockSpec(memory_space=pltpu.VMEM)
    smem = pl.BlockSpec(memory_space=pltpu.SMEM)
    many = isinstance(out_shape, (tuple, list))
    return pl.pallas_call(
        kernel,
        out_shape=out_shape,
        in_specs=[smem] * n_scalar + [vmem] * n_in,
        out_specs=tuple(vmem for _ in out_shape) if many else vmem,
        scratch_shapes=list(scratch),
        name=name,
        compiler_params=pltpu.CompilerParams(vmem_limit_bytes=48 * 1024 * 1024),
    )


def ring(block, axis, size, distance):
    return lax.ppermute(block, axis, [((i + distance) % size, i) for i in range(size)])


def per_device(images, kernel, cotangent):
    S = jax.ShapeDtypeStruct
    x, zl = lax.axis_index("x"), lax.axis_index("zl")
    core = lax.axis_index("core")
    space = lax.axis_index(("y", "zh", "core"))
    n_space = 32
    images, cotangent = images[0], cotangent[0]
    low = lax.ppermute(cotangent[0], ("y", "zh", "core"), [(i + 1, i) for i in range(n_space - 1)])
    up = lax.ppermute(images[ROWS - 1], ("y", "zh", "core"), [(i, i + 1) for i in range(n_space - 1)])
    panel = lax.dynamic_index_in_dim(kernel.reshape(16, 9, 2, CH // 2), core, 2, keepdims=False)
    panel = panel.reshape(16, 9 * CH // 2)
    zs = jnp.concatenate([panel] + [ring(panel, "zl", 4, d) for d in (1, 3, 2)], axis=0)
    mine = jnp.concatenate([zs] + [ring(zs, "x", 4, d) for d in (1, 3, 2)], axis=0)
    swap = [(0, 1), (1, 0)]
    other = lax.ppermute(mine, "core", swap)

    keep, send, ee, eo, oe, oo, cot_s = call(
        wgrad_kernel,
        "wgrad",
        (S((16, 9, 16, 128), F32), S((16, 9, 16, 128), BF), S((POS, CH), BF), S((POS, CH), BF),
         S((POS, CH), BF), S((POS, CH), BF), S((POS + Q, CH), BF)),
        scratch=[pltpu.VMEM((4, POS, CH), BF), pltpu.VMEM((4, CH, POS), BF)],
        n_scalar=1,
        n_in=3,
    )(core.astype(jnp.int32).reshape(1), images, cotangent, low)
    recv = lax.ppermute(send, "core", swap)
    both = (keep + recv.astype(F32)).astype(BF).reshape(4, 576, 128)
    parts = lax.all_to_all(both, "x", 0, 0, tiled=True)
    turned = call(sum_kernel, "sum_x", S((16, 4, 8, 144), BF), n_in=1)(parts)
    pieces = lax.all_to_all(turned.reshape(64, 8, 144), ("y", "zh", "zl"), 0, 0, tiled=True)

    place = jnp.stack([core, x, zl, space]).astype(jnp.int32)
    output, grad_input, pen, rows = call(
        conv_kernel,
        "conv",
        (S((R, Q, CH), BF), S((ROWS, COLS, CH), BF), S((8, 144), F32), S((16, 1), F32)),
        scratch=[pltpu.VMEM((CH, 9 * CH), BF), pltpu.VMEM((4, POS, CH), F32), pltpu.VMEM((POS, CH), F32)],
        n_scalar=1,
        n_in=10,
    )(place, mine, other, up, low, cotangent, cot_s, ee, eo, oe, oo)
    own = jnp.sum(pieces.astype(F32), axis=0) / (R * n_space) + (4.0 * PEN_WEIGHT) * pen
    grad_kernel = jnp.transpose(own.reshape(8, 9, 16), (2, 1, 0)).reshape(16, 3, 3, 8)
    return output[None], grad_input[None], grad_kernel, rows.reshape(16)


def solution(mesh):
    fine = Mesh(mesh.devices.reshape(4, 4, 8, 2, 2), ("x", "zl", "y", "zh", "core"))
    fsdp, space = ("x", "zl"), ("y", "zh", "core")
    in_specs = (
        P(fsdp, space, None, None),
        P(fsdp, None, None, None),
        P(fsdp, space, None, None),
    )
    out_specs = (
        P(fsdp, space, None, None),
        P(fsdp, space, None, None),
        P(fsdp, None, None, space),
        P(fsdp),
    )
    return jax.shard_map(
        per_device, mesh=fine, in_specs=in_specs, out_specs=out_specs, check_vma=False
    )
```

time: 335 us -> 96.9 us (0.29)
  the two profiles are of different devices: /device:TPU:6 before, /device:TPU:32 now
where the time goes in v1:
time: 96.9 us; the launch traced here: 96.1 us
  starting transfers between devices  52.6 us (54%)
  waiting for transfers between devices  25.5 us (26%)
  Pallas kernels  8.47 us (9%)
  local copies, waits for them, and re-layouts  6.92 us (7%)
  other arithmetic  1.72 us (2%)
    ppermute x6, starting transfers between devices, ring(): lax.ppermute(block, axis, [((i + distance) % size, i) for i in range(size)])  24.2 us
    all_to_all x1, starting transfers between devices, per_device(): lax.all_to_all(turned.reshape(64, 8, 144), ('y', 'zh', 'zl'), 0, 0, tiled...  11.5 us
    ppermute x1, waiting for transfers between devices, per_device(): lax.ppermute(images[ROWS - 1], ('y', 'zh', 'core'), [(i, i + 1) for i in...  10.3 us
    all_to_all x1, waiting for transfers between devices, per_device(): parts = lax.all_to_all(both, 'x', 0, 0, tiled=True)  8.32 us
    ppermute x1, starting transfers between devices, per_device(): lax.ppermute(cotangent[0], ('y', 'zh', 'core'), [(i + 1, i) for i in rang...  7.59 us
    ppermute x6, waiting for transfers between devices, ring(): lax.ppermute(block, axis, [((i + distance) % size, i) for i in range(size)])  6.92 us
    pallas_call x1, Pallas kernels, per_device(): call(conv_kernel, 'conv', (S((R, Q, CH), BF), S((ROWS, COLS, CH), BF), S(...  5.44 us
    unnamed x19, local copies, waits for them, and re-layouts  3.53 us
  transfers between devices with their start and end apart: 12, of which 3 were waited for; matrix products, arithmetic and copies ran while one was open for 3% of the time, Pallas kernels for 9%

profile of v1, /device:TPU:32, one launch (start us, length us, event | category | flops | bytes accessed | tf_op | source)
XLA Modules:
  0.0 96.1 jit_solution(9475902404561017908)
XLA Ops:
  0.6 0.0 copy-start.1
  0.6 1.0 reshape.35
  1.6 0.1 constant_dynamic-slice_fusion
  1.8 6.1 %collective-permute-start.2 = (bf16[16,1152]{1,0:T(8,128)(2,1)S(1)}, bf16[16,1152]{1,0:T(8,128)(2,1)S(1)}, u32[]{:S(2)}, u32[]{:S(2)}) collective-permute-start(bf16[16,1152]{1,0:T(8,128)(2,1)S(1)} %get-tuple-element.31), channel_id=1, source_target_pairs={{64,0},{96,32},{0,64},{32,96},{65,1},{97,33},{1,65},{33,97},{66,2}... | collective-permute-start | bytes 110600 | tf_op jit(solution)/shard_map/ppermute | solution.py:221
  7.8 4.3 %collective-permute-start.1 = (bf16[16,1152]{1,0:T(8,128)(2,1)S(1)}, bf16[16,1152]{1,0:T(8,128)(2,1)S(1)}, u32[]{:S(2)}, u32[]{:S(2)}) collective-permute-start(bf16[16,1152]{1,0:T(8,128)(2,1)S(1)} %get-tuple-element.31), channel_id=1, source_target_pairs={{96,0},{0,32},{32,64},{64,96},{97,1},{1,33},{33,65},{65,97},{98,2}... | collective-permute-start | bytes 110600 | tf_op jit(solution)/shard_map/ppermute | solution.py:221
  12.1 3.4 %collective-permute-start = (bf16[16,1152]{1,0:T(8,128)(2,1)S(1)}, bf16[16,1152]{1,0:T(8,128)(2,1)S(1)}, u32[]{:S(2)}, u32[]{:S(2)}) collective-permute-start(bf16[16,1152]{1,0:T(8,128)(2,1)S(1)} %get-tuple-element.31), channel_id=1, source_target_pairs={{32,0},{64,32},{96,64},{0,96},{33,1},{65,33},{97,65},{1,97},{34,2}... | collective-permute-start | bytes 110600 | tf_op jit(solution)/shard_map/ppermute | solution.py:221
  15.5 0.8 slice_bitcast_fusion.1
  16.3 7.6 %collective-permute-start.8 = (bf16[64,256]{1,0:T(8,128)(2,1)S(1)}, bf16[64,256]{1,0:T(8,128)(2,1)S(1)}, u32[]{:S(2)}, u32[]{:S(2)}) collective-permute-start(bf16[64,256]{1,0:T(8,128)(2,1)S(1)} %slice_bitcast_fusion.1), channel_id=1, source_target_pairs={{1,0},{2,1},{3,2},{4,3},{5,4},{6,5},{7,6},{8,7},{9,8},{10,9},{11,1... | collective-permute-start | bytes 98312 | tf_op jit(solution)/shard_map/ppermute | solution.py:231
  24.0 4.7 %collective-permute-start.3 = (bf16[64,1152]{1,0:T(8,128)(2,1)S(1)}, bf16[64,1152]{1,0:T(8,128)(2,1)S(1)}, u32[]{:S(2)}, u32[]{:S(2)}) collective-permute-start(bf16[64,1152]{1,0:T(8,128)(2,1)S(1)} %get-tuple-element.32), channel_id=1, source_target_pairs={{128,0},{256,128},{384,256},{0,384},{129,1},{257,129},{385,257},{1... | collective-permute-start | bytes 442376 | tf_op jit(solution)/shard_map/ppermute | solution.py:221
  28.7 1.4 %copy-done = bf16[1,24,128,256]{3,2,1,0:T(8,128)(2,1)S(1)} copy-done((bf16[1,24,128,256]{3,2,1,0:T(8,128)(2,1)S(1)}, bf16[1,24,128,256]{3,2,1,0:T(8,128)(2,1)}, u32[]{:S(2)}) %copy-start) | copy-done | bytes 1572888
  30.1 2.1 %wgrad.1 = (f32[16,9,16,128]{3,2,1,0:T(8,128)S(1)}, bf16[16,9,16,128]{3,2,1,0:T(8,128)(2,1)S(1)}, bf16[768,256]{1,0:T(8,128)(2,1)S(1)}, bf16[768,256]{1,0:T(8,12...) custom-call(s32[1]{0:T(128)} %bitcast.core_ref, ...), custom_call_target="tpu_custom_call" | custom-call | tf_op jit(solution)/shard_map/wgrad/pallas_call | solution.py:240
  32.2 1.9 %collective-permute-start.9 = (bf16[16,9,16,128]{3,2,1,0:T(8,128)(2,1)S(1)}, bf16[16,9,16,128]{3,2,1,0:T(8,128)(2,1)S(1)}, u32[]{:S(2)}, u32[]{:S(2)}) collective-permute-start(bf16[16,9,16,128]{3,2,1,0:T(8,128)(2,1)S(1)} %get-tuple-element.23), channel_id=1, source_target_pairs={{0,1},{1,0},{2,3},{3,2},{4,5},{5,4},{6,7},{7,6},{8,9},{9,8},{10,11... | collective-permute-start | bytes 1769480 | tf_op jit(solution)/shard_map/ppermute | solution.py:249
  34.1 3.3 %collective-permute-start.5 = (bf16[64,1152]{1,0:T(8,128)(2,1)S(1)}, bf16[64,1152]{1,0:T(8,128)(2,1)S(1)}, u32[]{:S(2)}, u32[]{:S(2)}) collective-permute-start(bf16[64,1152]{1,0:T(8,128)(2,1)S(1)} %get-tuple-element.32), channel_id=1, source_target_pairs={{256,0},{384,128},{0,256},{128,384},{257,1},{385,129},{1,257},{129... | collective-permute-start | bytes 442376 | tf_op jit(solution)/shard_map/ppermute | solution.py:221
  37.5 2.5 %collective-permute-start.4 = (bf16[64,1152]{1,0:T(8,128)(2,1)S(1)}, bf16[64,1152]{1,0:T(8,128)(2,1)S(1)}, u32[]{:S(2)}, u32[]{:S(2)}) collective-permute-start(bf16[64,1152]{1,0:T(8,128)(2,1)S(1)} %get-tuple-element.32), channel_id=1, source_target_pairs={{384,0},{0,128},{128,256},{256,384},{385,1},{1,129},{129,257},{257... | collective-permute-start | bytes 442376 | tf_op jit(solution)/shard_map/ppermute | solution.py:221
  40.0 6.9 %collective-permute-done.4 = bf16[64,1152]{1,0:T(8,128)(2,1)S(1)} collective-permute-done((bf16[64,1152]{1,0:T(8,128)(2,1)S(1)}, bf16[64,1152]{1,0:T(8,128)(2,1)S(1)}, u32[]{:S(2)}, u32[]{:S(2)}) %collective-permute-start.4) | collective-permute-done | bytes 147488 | tf_op jit(solution)/shard_map/ppermute | solution.py:221
  47.0 0.9 add_convert_fusion
  47.9 3.5 %all-to-all-start = ((bf16[4,576,128]{2,1,0:T(8,128)(2,1)}), bf16[4,576,128]{2,1,0:T(8,128)(2,1)S(1)}, u32[]{:S(2)}, u32[]{:S(2)}) async-start(bf16[4,576,128]{2,1,0:T(8,128)(2,1)} %bitcast.10), calls=%async_computation | async-start | bytes 1179648 | tf_op jit(solution)/shard_map/all_to_all | solution.py:251
  51.4 1.9 %collective-permute-start.6 = (bf16[256,1152]{1,0:T(8,128)(2,1)S(1)}, bf16[256,1152]{1,0:T(8,128)(2,1)S(1)}, u32[]{:S(2)}, u32[]{:S(2)}) collective-permute-start(bf16[256,1152]{1,0:T(8,128)(2,1)S(1)} %constant_dynamic-update-slice_fusion.4.mine_ref), channel_id=1, source_target_pairs={{0,1},{1,0},{2,3},{3,2},{4,5},{5,4},{6,7},{7,6},{8,9},{9,8},{10,11... | collective-permute-start | bytes 1769480 | tf_op jit(solution)/shard_map/ppermute | solution.py:238
  53.4 8.3 %all-to-all-done.parts_ref = bf16[4,576,128]{2,1,0:T(8,128)(2,1)S(1)} async-done(((bf16[4,576,128]{2,1,0:T(8,128)(2,1)}), bf16[4,576,128]{2,1,0:T(8,128)(2,1)S(1)}, u32[]{:S(2)}, u32[]{:S(2)}) %all-to-all-start) | async-done | bytes 589856 | tf_op jit(solution)/shard_map/all_to_all | solution.py:251
  61.7 0.9 sum_x.1
  62.6 11.5 %all-to-all-start.1 = ((bf16[64,8,144]{2,1,0:T(8,128)(2,1)}), bf16[64,8,144]{2,1,0:T(8,128)(2,1)S(1)}, u32[]{:S(2)}, u32[]{:S(2)}) async-start(bf16[64,8,144]{2,1,0:T(8,128)(2,1)} %bitcast.11), calls=%async_computation.1 | async-start | bytes 524288 | tf_op jit(solution)/shard_map/all_to_all | solution.py:253
  74.2 0.8 slice_bitcast_fusion
  75.0 1.9 %collective-permute-start.7 = (bf16[128,256]{1,0:T(8,128)(2,1)S(1)}, bf16[128,256]{1,0:T(8,128)(2,1)S(1)}, u32[]{:S(2)}, u32[]{:S(2)}) collective-permute-start(bf16[128,256]{1,0:T(8,128)(2,1)S(1)} %slice_bitcast_fusion), channel_id=1, source_target_pairs={{0,1},{1,2},{2,3},{3,4},{4,5},{5,6},{6,7},{7,8},{8,9},{9,10},{10,1... | collective-permute-start | bytes 196616 | tf_op jit(solution)/shard_map/ppermute | solution.py:232
  76.9 0.1 pad_add_fusion.place_ref
  77.0 10.3 %collective-permute-done.7.up_ref = bf16[128,256]{1,0:T(8,128)(2,1)S(1)} collective-permute-done((bf16[128,256]{1,0:T(8,128)(2,1)S(1)}, bf16[128,256]{1,0:T(8,128)(2,1)S(1)}, u32[]{:S(2)}, u32[]{:S(2)}) %collective-permute-start.7) | collective-permute-done | bytes 65568 | tf_op jit(solution)/shard_map/ppermute | solution.py:232
  87.3 1.0 %copy-done.3 = bf16[768,256]{1,0:T(8,128)(2,1)S(1)} copy-done((bf16[768,256]{1,0:T(8,128)(2,1)S(1)}, bf16[768,256]{1,0:T(8,128)(2,1)}, u32[]{:S(2)}) %copy-start.3) | copy-done | bytes 393240
  88.3 1.0 %copy-done.5 = bf16[768,256]{1,0:T(8,128)(2,1)S(1)} copy-done((bf16[768,256]{1,0:T(8,128)(2,1)S(1)}, bf16[768,256]{1,0:T(8,128)(2,1)}, u32[]{:S(2)}) %copy-start.5) | copy-done | bytes 393240
  89.3 5.4 %conv.1 = (bf16[12,64,256]{2,1,0:T(8,128)(2,1)}, bf16[24,128,256]{2,1,0:T(8,128)(2,1)}, f32[8,144]{1,0:T(8,128)S(1)}, f32[16,1]{1,0:T(8,128)S(1)}) custom-call(s32[4]{0:T(128)S(1)} %pad_add_fusion.place_ref, bf16[256,1152]{1,0:T(8,128)(2,1)S(1)} %constant_dynamic-update-slice_fusion.4.mine_ref, bf16[256,1152]{1,0:T(8,128)(2,1)S(1)} %collective-permute-done.6.other_ref, ...), custom_call_target="tpu_custom_call" | custom-call | tf_op jit(solution)/shard_map/conv/pallas_call | solution.py:256
  94.7 0.6 reduce
  95.3 0.1 convert_reduce_fusion
  95.4 0.1 reshape.39
  95.5 0.6 copy.12
  (27 shorter events, 0.2 us)
Async XLA Ops:
  0.6 28.0 %copy-start.1 = (bf16[1,12,64,256]{3,2,1,0:T(8,128)(2,1)S(1)}, bf16[1,12,64,256]{3,2,1,0:T(8,128)(2,1)}, u32[]{:S(2)}) copy-start(bf16[1,12,64,256]{3,2,1,0:T(8,128)(2,1)} %param.5) | copy-start | bytes 1179652
  1.8 22.2 %collective-permute-start.2 = (bf16[16,1152]{1,0:T(8,128)(2,1)S(1)}, bf16[16,1152]{1,0:T(8,128)(2,1)S(1)}, u32[]{:S(2)}, u32[]{:S(2)}) collective-permute-start(bf16[16,1152]{1,0:T(8,128)(2,1)S(1)} %get-tuple-element.31), channel_id=1, source_target_pairs={{64,0},{96,32},{0,64},{32,96},{65,1},{97,33},{1,65},{33,97},{66,2}... | collective-permute-start | bytes 110600 | tf_op jit(solution)/shard_map/ppermute | solution.py:221
  7.8 16.1 %collective-permute-start.1 = (bf16[16,1152]{1,0:T(8,128)(2,1)S(1)}, bf16[16,1152]{1,0:T(8,128)(2,1)S(1)}, u32[]{:S(2)}, u32[]{:S(2)}) collective-permute-start(bf16[16,1152]{1,0:T(8,128)(2,1)S(1)} %get-tuple-element.31), channel_id=1, source_target_pairs={{96,0},{0,32},{32,64},{64,96},{97,1},{1,33},{33,65},{65,97},{98,2}... | collective-permute-start | bytes 110600 | tf_op jit(solution)/shard_map/ppermute | solution.py:221
  12.1 11.7 %collective-permute-start = (bf16[16,1152]{1,0:T(8,128)(2,1)S(1)}, bf16[16,1152]{1,0:T(8,128)(2,1)S(1)}, u32[]{:S(2)}, u32[]{:S(2)}) collective-permute-start(bf16[16,1152]{1,0:T(8,128)(2,1)S(1)} %get-tuple-element.31), channel_id=1, source_target_pairs={{32,0},{64,32},{96,64},{0,96},{33,1},{65,33},{97,65},{1,97},{34,2}... | collective-permute-start | bytes 110600 | tf_op jit(solution)/shard_map/ppermute | solution.py:221
  16.3 12.4 %collective-permute-start.8 = (bf16[64,256]{1,0:T(8,128)(2,1)S(1)}, bf16[64,256]{1,0:T(8,128)(2,1)S(1)}, u32[]{:S(2)}, u32[]{:S(2)}) collective-permute-start(bf16[64,256]{1,0:T(8,128)(2,1)S(1)} %slice_bitcast_fusion.1), channel_id=1, source_target_pairs={{1,0},{2,1},{3,2},{4,3},{5,4},{6,5},{7,6},{8,7},{9,8},{10,9},{11,1... | collective-permute-start | bytes 98312 | tf_op jit(solution)/shard_map/ppermute | solution.py:231
  24.0 16.0 %collective-permute-start.3 = (bf16[64,1152]{1,0:T(8,128)(2,1)S(1)}, bf16[64,1152]{1,0:T(8,128)(2,1)S(1)}, u32[]{:S(2)}, u32[]{:S(2)}) collective-permute-start(bf16[64,1152]{1,0:T(8,128)(2,1)S(1)} %get-tuple-element.32), channel_id=1, source_target_pairs={{128,0},{256,128},{384,256},{0,384},{129,1},{257,129},{385,257},{1... | collective-permute-start | bytes 442376 | tf_op jit(solution)/shard_map/ppermute | solution.py:221
  28.7 1.4 %copy-start = (bf16[1,24,128,256]{3,2,1,0:T(8,128)(2,1)S(1)}, bf16[1,24,128,256]{3,2,1,0:T(8,128)(2,1)}, u32[]{:S(2)}) copy-start(bf16[1,24,128,256]{3,2,1,0:T(8,128)(2,1)} %param.3) | copy-start | bytes 4718596
  32.2 15.7 %copy-start.2 = (bf16[768,256]{1,0:T(8,128)(2,1)}, bf16[768,256]{1,0:T(8,128)(2,1)S(1)}, u32[]{:S(2)}) copy-start(bf16[768,256]{1,0:T(8,128)(2,1)S(1)} %get-tuple-element.18.oe_ref) | copy-start | bytes 1179652
  32.2 15.7 %copy-start.4 = (bf16[768,256]{1,0:T(8,128)(2,1)}, bf16[768,256]{1,0:T(8,128)(2,1)S(1)}, u32[]{:S(2)}) copy-start(bf16[768,256]{1,0:T(8,128)(2,1)S(1)} %get-tuple-element.19.oo_ref) | copy-start | bytes 1179652
  32.2 14.8 %collective-permute-start.9 = (bf16[16,9,16,128]{3,2,1,0:T(8,128)(2,1)S(1)}, bf16[16,9,16,128]{3,2,1,0:T(8,128)(2,1)S(1)}, u32[]{:S(2)}, u32[]{:S(2)}) collective-permute-start(bf16[16,9,16,128]{3,2,1,0:T(8,128)(2,1)S(1)} %get-tuple-element.23), channel_id=1, source_target_pairs={{0,1},{1,0},{2,3},{3,2},{4,5},{5,4},{6,7},{7,6},{8,9},{9,8},{10,11... | collective-permute-start | bytes 1769480 | tf_op jit(solution)/shard_map/ppermute | solution.py:249
  34.1 17.3 %collective-permute-start.5 = (bf16[64,1152]{1,0:T(8,128)(2,1)S(1)}, bf16[64,1152]{1,0:T(8,128)(2,1)S(1)}, u32[]{:S(2)}, u32[]{:S(2)}) collective-permute-start(bf16[64,1152]{1,0:T(8,128)(2,1)S(1)} %get-tuple-element.32), channel_id=1, source_target_pairs={{256,0},{384,128},{0,256},{128,384},{257,1},{385,129},{1,257},{129... | collective-permute-start | bytes 442376 | tf_op jit(solution)/shard_map/ppermute | solution.py:221
  37.5 9.5 %collective-permute-start.4 = (bf16[64,1152]{1,0:T(8,128)(2,1)S(1)}, bf16[64,1152]{1,0:T(8,128)(2,1)S(1)}, u32[]{:S(2)}, u32[]{:S(2)}) collective-permute-start(bf16[64,1152]{1,0:T(8,128)(2,1)S(1)} %get-tuple-element.32), channel_id=1, source_target_pairs={{384,0},{0,128},{128,256},{256,384},{385,1},{1,129},{129,257},{257... | collective-permute-start | bytes 442376 | tf_op jit(solution)/shard_map/ppermute | solution.py:221
  47.9 13.8 %all-to-all-start = ((bf16[4,576,128]{2,1,0:T(8,128)(2,1)}), bf16[4,576,128]{2,1,0:T(8,128)(2,1)S(1)}, u32[]{:S(2)}, u32[]{:S(2)}) async-start(bf16[4,576,128]{2,1,0:T(8,128)(2,1)} %bitcast.10), calls=%async_computation | async-start | bytes 1179648 | tf_op jit(solution)/shard_map/all_to_all | solution.py:251
  51.4 35.9 %collective-permute-start.6 = (bf16[256,1152]{1,0:T(8,128)(2,1)S(1)}, bf16[256,1152]{1,0:T(8,128)(2,1)S(1)}, u32[]{:S(2)}, u32[]{:S(2)}) collective-permute-start(bf16[256,1152]{1,0:T(8,128)(2,1)S(1)} %constant_dynamic-update-slice_fusion.4.mine_ref), channel_id=1, source_target_pairs={{0,1},{1,0},{2,3},{3,2},{4,5},{5,4},{6,7},{7,6},{8,9},{9,8},{10,11... | collective-permute-start | bytes 1769480 | tf_op jit(solution)/shard_map/ppermute | solution.py:238
  62.6 32.7 %all-to-all-start.1 = ((bf16[64,8,144]{2,1,0:T(8,128)(2,1)}), bf16[64,8,144]{2,1,0:T(8,128)(2,1)S(1)}, u32[]{:S(2)}, u32[]{:S(2)}) async-start(bf16[64,8,144]{2,1,0:T(8,128)(2,1)} %bitcast.11), calls=%async_computation.1 | async-start | bytes 524288 | tf_op jit(solution)/shard_map/all_to_all | solution.py:253
  75.0 12.3 %collective-permute-start.7 = (bf16[128,256]{1,0:T(8,128)(2,1)S(1)}, bf16[128,256]{1,0:T(8,128)(2,1)S(1)}, u32[]{:S(2)}, u32[]{:S(2)}) collective-permute-start(bf16[128,256]{1,0:T(8,128)(2,1)S(1)} %slice_bitcast_fusion), channel_id=1, source_target_pairs={{0,1},{1,2},{2,3},{3,4},{4,5},{5,6},{6,7},{7,8},{8,9},{9,10},{10,1... | collective-permute-start | bytes 196616 | tf_op jit(solution)/shard_map/ppermute | solution.py:232
  87.3 1.0 %copy-start.3 = (bf16[768,256]{1,0:T(8,128)(2,1)S(1)}, bf16[768,256]{1,0:T(8,128)(2,1)}, u32[]{:S(2)}) copy-start(bf16[768,256]{1,0:T(8,128)(2,1)} %copy-done.2) | copy-start | bytes 1179652
  88.3 1.0 %copy-start.5 = (bf16[768,256]{1,0:T(8,128)(2,1)S(1)}, bf16[768,256]{1,0:T(8,128)(2,1)}, u32[]{:S(2)}) copy-start(bf16[768,256]{1,0:T(8,128)(2,1)} %copy-done.4) | copy-start | bytes 1179652

commit v2 on v1

v2 whole, which is shorter than its diff:
```python
import jax
import jax.numpy as jnp
from jax import lax
from jax.experimental import pallas as pl
from jax.experimental.pallas import tpu as pltpu
from jax.sharding import Mesh, PartitionSpec as P

PEN_WEIGHT = 4.0
BF = jnp.bfloat16
F32 = jnp.float32

ROWS, COLS, CH = 24, 128, 256
R, Q = 12, 64
POS = R * Q
TAPS = [(i, j) for i in range(3) for j in range(3)]
SHIFTS = [(u, v) for u in (-2, 0, 2) for v in (-2, 0, 2)]

NT = (((1,), (1,)), ((), ()))


def mm(a, b):
    return jnp.dot(a, b, preferred_element_type=F32)


def mm_nt(a, b):
    return lax.dot_general(a, b, NT, preferred_element_type=F32)


def one_hot(cond):
    return jnp.where(cond, 1.0, 0.0).astype(BF)


def iota2(shape, axis):
    return lax.broadcasted_iota(jnp.int32, shape, axis)


def column_sorter():
    row, col = iota2((COLS, COLS), 0), iota2((COLS, COLS), 1)
    return one_hot(col == 2 * (row % Q) + row // Q)


def shift_left(block):
    moved = pltpu.roll(block, Q - 1, 0)
    return jnp.where(iota2(block.shape, 0) == Q - 1, 0.0, moved)


def shift_right(block):
    moved = pltpu.roll(block, 1, 0)
    return jnp.where(iota2(block.shape, 0) == 0, 0.0, moved)


def prep_kernel(
    core_ref, img_ref, cot_ref,
    per_ref, turn_ref, turn_low_ref,
    cot_s_ref,
):
    core = core_ref[0]
    sorter = column_sorter()
    chan, slot = iota2((CH, CH), 0), iota2((CH, CH), 1)
    other = jnp.where((chan // 8) % 2 == core, 0, 1)
    to_core = one_hot(slot == (chan // 16) * 8 + chan % 8 + (CH // 2) * other)
    for r in range(R):
        for parity in range(2):
            split = mm(sorter, img_ref[2 * r + parity]).astype(BF)
            per_ref[2 * parity, r * Q : (r + 1) * Q] = split[:Q]
            per_ref[2 * parity + 1, r * Q : (r + 1) * Q] = split[Q:]
    for k in range(4):
        per_ref[k] = mm(per_ref[k], to_core).astype(BF)
    for r in range(R):
        cot_s_ref[r * Q : (r + 1) * Q] = shift_left(cot_ref[r].astype(F32)).astype(BF)
    turn_ref[0] = cot_ref[...].reshape(POS, CH).T
    turn_ref[1] = cot_s_ref[...].T
    turn_low_ref[0] = cot_ref[1:].reshape(POS - Q, CH).T
    turn_low_ref[1] = cot_s_ref[Q:].T


def wgrad_kernel(low_ref, per_ref, turn_ref, turn_low_ref, keep_ref, send_ref):
    low = low_ref[...].astype(F32)
    low_t = (low.T.astype(BF), shift_left(low).T.astype(BF))
    for t, (i, j) in enumerate(TAPS):
        moved = 1 if j == 0 else 0
        image = (0 if i == 1 else 2) + (0 if j == 1 else 1)
        if i == 0:
            tap = mm(turn_low_ref[moved], per_ref[image, : POS - Q]) + mm(low_t[moved], per_ref[image, POS - Q :])
        else:
            tap = mm(turn_ref[moved], per_ref[image])
        tap = tap.reshape(16, 16, CH)
        keep_ref[:, t] = tap[:, :, : CH // 2]
        send_ref[:, t] = tap[:, :, CH // 2 :].astype(BF)


def back_kernel(
    place_ref, mine_ref, other_ref, low_ref, cot_ref,
    gin_ref, w_ref, pen_ref, row_ref,
    acc_ref, cot_s_ref,
):
    core, x, zl, space = place_ref[0], place_ref[1], place_ref[2], place_ref[3]
    half = CH // 2

    def halves(lower_ref, upper_ref):
        for t in range(9):
            lanes = slice(t * half, (t + 1) * half)
            w_ref[:, t * CH : t * CH + half] = lower_ref[:, lanes]
            w_ref[:, t * CH + half : (t + 1) * CH] = upper_ref[:, lanes]

    @pl.when(core == 0)
    def _():
        halves(mine_ref, other_ref)

    @pl.when(core == 1)
    def _():
        halves(other_ref, mine_ref)

    def tap(i, j):
        t = 3 * i + j
        return w_ref[:, t * CH : (t + 1) * CH]

    cot = cot_ref[...].reshape(POS, CH)
    below = jnp.concatenate([cot[Q:], low_ref[...]], axis=0)
    for r in range(R):
        cot_s_ref[r * Q : (r + 1) * Q] = shift_left(cot_ref[r].astype(F32)).astype(BF)
    cot_s = cot_s_ref[...]
    below_s = jnp.concatenate([cot_s[Q:], shift_left(low_ref[...].astype(F32)).astype(BF)], axis=0)
    acc_ref[0] = mm(cot, tap(1, 1))
    acc_ref[1] = mm(cot, tap(1, 2))
    acc_ref[1] += mm(cot_s, tap(1, 0))
    acc_ref[2] = mm(cot, tap(2, 1))
    acc_ref[2] += mm(below, tap(0, 1))
    acc_ref[3] = mm(cot, tap(2, 2))
    acc_ref[3] += mm(cot_s, tap(2, 0))
    acc_ref[3] += mm(below, tap(0, 2))
    acc_ref[3] += mm(below_s, tap(0, 0))
    row, col = iota2((COLS, COLS), 0), iota2((COLS, COLS), 1)
    weaver = one_hot(col == (row % 2) * Q + row // 2)
    for r in range(R):
        rows = slice(r * Q, (r + 1) * Q)
        for parity in range(2):
            both = jnp.concatenate(
                [acc_ref[2 * parity, rows].astype(BF), acc_ref[2 * parity + 1, rows].astype(BF)], axis=0
            )
            gin_ref[2 * r + parity] = mm(weaver, both).astype(BF)
    own_first = pl.multiple_of((x * 4 + zl) * 16, 16)
    own = [w_ref[pl.ds(own_first, 16), t * CH : (t + 1) * CH] for t in range(9)]
    grams = {}
    kin = [[s for s in range(9) if (s // 3 - t // 3) % 2 == 0 and (s % 3 - t % 3) % 2 == 0] for t in range(9)]
    for t in range(9):
        stacked = jnp.concatenate([own[s] for s in kin[t]], axis=0)
        part = mm_nt(stacked, w_ref[:, t * CH : (t + 1) * CH])
        for n, s in enumerate(kin[t]):
            shift = (s // 3 - t // 3, s % 3 - t % 3)
            block = part[n * 16 : (n + 1) * 16]
            grams[shift] = grams[shift] + block if shift in grams else block
    diagonal = iota2((16, CH), 0) + own_first == iota2((16, CH), 1)
    grams[(0, 0)] = grams[(0, 0)] - jnp.where(diagonal, 1.0, 0.0)
    squares = jnp.zeros((16, CH), F32)
    for shift in SHIFTS:
        squares = squares + grams[shift] * grams[shift]
    row_ref[...] = jnp.sum(squares.T, axis=0, keepdims=True)
    pieces = {}
    for shift in SHIFTS:
        high = grams[shift].astype(BF)
        rest = grams[shift] - high.astype(F32)
        pieces[shift] = (high, rest.astype(BF))
    grads = [jnp.zeros((16, CH), F32) for _ in range(9)]
    for s in range(9):
        stacked = jnp.concatenate(
            [pieces[(t // 3 - s // 3, t % 3 - s % 3)][p] for t in kin[s] for p in range(2)], axis=0
        )
        part = mm(stacked, w_ref[:, s * CH : (s + 1) * CH])
        for n, t in enumerate(kin[s]):
            for p in range(2):
                grads[t] = grads[t] + part[(2 * n + p) * 16 : (2 * n + p + 1) * 16]
    stacked = jnp.concatenate(grads, axis=0)
    high = stacked.astype(BF)
    rest = stacked - high.astype(F32)
    mid = rest.astype(BF)
    low = (rest - mid.astype(F32)).astype(BF)
    pick = one_hot(iota2((8, CH), 0) + space * 8 == iota2((8, CH), 1))
    pen_ref[...] = mm_nt(pick, high) + mm_nt(pick, mid) + mm_nt(pick, low)


def fore_kernel(w_ref, up_ref, img_ref, out_ref, ee_ref, eo_ref, oe_ref, oo_ref, acc_ref, z_ref):
    def tap(i, j):
        t = 3 * i + j
        return w_ref[:, t * CH : (t + 1) * CH]

    sorter = column_sorter()
    for r in range(R):
        rows = slice(r * Q, (r + 1) * Q)
        for parity, (even_ref, odd_ref) in enumerate(((ee_ref, eo_ref), (oe_ref, oo_ref))):
            split = mm(sorter, img_ref[2 * r + parity]).astype(BF)
            even_ref[rows] = split[:Q]
            odd_ref[rows] = split[Q:]
    halo = mm(sorter, up_ref[...]).astype(BF)
    oe_up = jnp.concatenate([halo[:Q], oe_ref[0 : POS - Q]], axis=0)
    oo_up = jnp.concatenate([halo[Q:], oo_ref[0 : POS - Q]], axis=0)
    z_ref[...] = mm_nt(eo_ref[...], tap(1, 0))
    z_ref[...] += mm_nt(oo_ref[...], tap(2, 0))
    z_ref[...] += mm_nt(oo_up, tap(0, 0))
    acc_ref[...] = mm_nt(ee_ref[...], tap(1, 1))
    acc_ref[...] += mm_nt(eo_ref[...], tap(1, 2))
    acc_ref[...] += mm_nt(oe_ref[...], tap(2, 1))
    acc_ref[...] += mm_nt(oo_ref[...], tap(2, 2))
    acc_ref[...] += mm_nt(oe_up, tap(0, 1))
    acc_ref[...] += mm_nt(oo_up, tap(0, 2))
    for r in range(R):
        rows = slice(r * Q, (r + 1) * Q)
        out_ref[r] = (acc_ref[rows] + shift_right(z_ref[rows])).astype(BF)


def sum_kernel(parts_ref, out_ref):
    total = parts_ref[0].astype(F32)
    for k in range(1, 4):
        total = total + parts_ref[k].astype(F32)
    turned = total.T
    for k in range(4):
        out_ref[:, k] = turned[:, 144 * k : 144 * (k + 1)].reshape(16, 8, 144).astype(BF)


def call(kernel, out_shape, scratch=(), n_scalar=0, n_in=0):
    vmem = pl.BlockSpec(memory_space=pltpu.VMEM)
    smem = pl.BlockSpec(memory_space=pltpu.SMEM)
    many = isinstance(out_shape, (tuple, list))
    return pl.pallas_call(
        kernel,
        out_shape=out_shape,
        in_specs=[smem] * n_scalar + [vmem] * n_in,
        out_specs=tuple(vmem for _ in out_shape) if many else vmem,
        scratch_shapes=list(scratch),
        compiler_params=pltpu.CompilerParams(vmem_limit_bytes=24 * 1024 * 1024),
    )


def spread(block, axis, size):
    return lax.all_to_all(jnp.broadcast_to(block[None], (size,) + block.shape), axis, 0, 0, tiled=True)


def per_device(images, kernel, cotangent):
    return body(images[0], kernel, cotangent[0])


def body(images, kernel, cotangent):
    S = jax.ShapeDtypeStruct
    core, x, zl = lax.axis_index("core"), lax.axis_index("x"), lax.axis_index("zl")
    space = lax.axis_index(("y", "zh", "core"))
    n_space = 32
    swap = [(0, 1), (1, 0)]
    panel = lax.dynamic_index_in_dim(kernel.reshape(16, 9, 2, CH // 2), core, 2, keepdims=False)
    own = spread(panel.reshape(16, 9 * CH // 2), "zl", 4).reshape(64, 9 * CH // 2)
    mine = spread(own, "x", 4).reshape(256, 9 * CH // 2)
    low = lax.ppermute(cotangent[0], ("y", "zh", "core"), [(i + 1, i) for i in range(n_space - 1)])
    per, turn, turn_low = call(
        prep_kernel,
        (S((4, POS, CH), BF), S((2, CH, POS), BF), S((2, CH, POS - Q), BF)),
        scratch=[pltpu.VMEM((POS, CH), BF)],
        n_scalar=1,
        n_in=2,
    )(core.astype(jnp.int32).reshape(1), images, cotangent)
    keep, send = call(
        wgrad_kernel, (S((16, 9, 16, 128), F32), S((16, 9, 16, 128), BF)), n_in=4
    )(low, per, turn, turn_low)
    recv = lax.ppermute(send, "core", swap)
    both = (keep + recv.astype(F32)).astype(BF).reshape(4, 576, 128)
    parts = lax.all_to_all(both, "x", 0, 0, tiled=True)
    turned = call(sum_kernel, S((16, 4, 8, 144), BF), n_in=1)(parts)
    pieces = lax.all_to_all(turned.reshape(64, 8, 144), ("y", "zh", "zl"), 0, 0, tiled=True)
    up = lax.ppermute(images[ROWS - 1], ("y", "zh", "core"), [(i, i + 1) for i in range(n_space - 1)])
    other = lax.ppermute(mine, "core", swap)
    place = jnp.stack([core, x, zl, space]).astype(jnp.int32)
    grad_input, whole, pen, rows = call(
        back_kernel,
        (S((ROWS, COLS, CH), BF), S((CH, 9 * CH), BF), S((8, 144), F32), S((1, 16), F32)),
        scratch=[pltpu.VMEM((4, POS, CH), F32), pltpu.VMEM((POS, CH), BF)],
        n_scalar=1,
        n_in=4,
    )(place, mine, other, low, cotangent)
    output = call(
        fore_kernel,
        S((R, Q, CH), BF),
        scratch=[pltpu.VMEM((POS, CH), BF)] * 4 + [pltpu.VMEM((POS, CH), F32)] * 2,
        n_in=3,
    )(whole, up, images)
    own = jnp.sum(pieces.astype(F32), axis=0) / (R * n_space) + (4.0 * PEN_WEIGHT) * pen
    grad_kernel = jnp.transpose(own.reshape(8, 9, 16), (2, 1, 0)).reshape(16, 3, 3, 8)
    return output[None], grad_input[None], grad_kernel, rows.reshape(16)


def solution(mesh):
    fine = Mesh(mesh.devices.reshape(4, 4, 8, 2, 2), ("x", "zl", "y", "zh", "core"))
    fsdp, space = ("x", "zl"), ("y", "zh", "core")
    in_specs = (
        P(fsdp, space, None, None),
        P(fsdp, None, None, None),
        P(fsdp, space, None, None),
    )
    out_specs = (
        P(fsdp, space, None, None),
        P(fsdp, space, None, None),
        P(fsdp, None, None, space),
        P(fsdp),
    )
    return jax.shard_map(
        per_device, mesh=fine, in_specs=in_specs, out_specs=out_specs, check_vma=False
    )
```

time: 96.9 us -> 87 us (0.90)
  the two profiles are of different devices: /device:TPU:32 before, /device:TPU:1 now
where the time goes in v2:
time: 87 us; the launch traced here: 86.4 us
  starting transfers between devices  48.9 us (56%)
  Pallas kernels  10.8 us (12%)
  waiting for transfers between devices  10.3 us (12%)
  blocking collectives  9.57 us (11%)
  local copies, waits for them, and re-layouts  4.91 us (6%)
  other arithmetic  1.09 us (1%)
    all_to_all x1, starting transfers between devices, body(): lax.all_to_all(turned.reshape(64, 8, 144), ('y', 'zh', 'zl'), 0, 0, tiled...  13.8 us
    ppermute x1, starting transfers between devices, body(): lax.ppermute(images[ROWS - 1], ('y', 'zh', 'core'), [(i, i + 1) for i in...  11.5 us
    all_to_all x1, blocking collectives, spread(): lax.all_to_all(jnp.broadcast_to(block[None], (size,) + block.shape), axis...  9.57 us
    ppermute x1, starting transfers between devices, body(): lax.ppermute(cotangent[0], ('y', 'zh', 'core'), [(i + 1, i) for i in rang...  8.73 us
    all_to_all x1, waiting for transfers between devices, spread(): lax.all_to_all(jnp.broadcast_to(block[None], (size,) + block.shape), axis...  6.84 us
    pallas_call x1, Pallas kernels, body(): call(back_kernel, (S((ROWS, COLS, CH), BF), S((CH, 9 * CH), BF), S((8, 14...  5.43 us
    ppermute x1, starting transfers between devices, body(): other = lax.ppermute(mine, 'core', swap)  5.27 us
    all_to_all x1, starting transfers between devices, spread(): lax.all_to_all(jnp.broadcast_to(block[None], (size,) + block.shape), axis...  4.01 us
  transfers between devices with their start and end apart: 7, of which 3 were waited for; matrix products, arithmetic and copies ran while one was open for 2% of the time, Pallas kernels for 11%

profile of v2, /device:TPU:1, one launch (start us, length us, event | category | flops | bytes accessed | tf_op | source)
XLA Modules:
  0.0 86.4 jit_solution(12686714942957447225)
XLA Ops:
  0.6 0.8 slice_bitcast_fusion.1
  1.4 8.7 %collective-permute-start.1 = (bf16[64,256]{1,0:T(8,128)(2,1)S(1)}, bf16[64,256]{1,0:T(8,128)(2,1)S(1)}, u32[]{:S(2)}, u32[]{:S(2)}) collective-permute-start(bf16[64,256]{1,0:T(8,128)(2,1)S(1)} %slice_bitcast_fusion.1), channel_id=1, source_target_pairs={{1,0},{2,1},{3,2},{4,3},{5,4},{6,5},{7,6},{8,7},{9,8},{10,9},{11,1... | collective-permute-start | bytes 98312 | tf_op jit(solution)/shard_map/ppermute | solution.py:251
  10.1 0.0 copy-start
  10.2 1.4 %copy-done = bf16[1,24,128,256]{3,2,1,0:T(8,128)(2,1)S(1)} copy-done((bf16[1,24,128,256]{3,2,1,0:T(8,128)(2,1)S(1)}, bf16[1,24,128,256]{3,2,1,0:T(8,128)(2,1)}, u32[]{:S(2)}) %copy-start) | copy-done | bytes 1572888
  11.6 1.0 %copy-done.2 = bf16[1,12,64,256]{3,2,1,0:T(8,128)(2,1)S(1)} copy-done((bf16[1,12,64,256]{3,2,1,0:T(8,128)(2,1)S(1)}, bf16[1,12,64,256]{3,2,1,0:T(8,128)(2,1)}, u32[]{:S(2)}) %copy-start.2) | copy-done | bytes 393240
  12.5 1.0 %shard_map.68 = (bf16[4,768,256]{2,1,0:T(8,128)(2,1)S(1)}, bf16[2,256,768]{2,1,0:T(8,128)(2,1)S(1)}, bf16[2,256,704]{2,1,0:T(8,128)(2,1)S(1)}) custom-call(s32[1]{0:T(128)} %bitcast.core_ref, bf16[24,128,256]{2,1,0:T(8,128)(2,1)S(1)} %bitcast.29, bf16[12,64,256]{2,1,0:T(8,128)(2,1)S(1)} %bitcast.33), custom_call_target="tpu_custom_call" | custom-call | tf_op jit(solution)/shard_map/pallas_call | solution.py:252
  13.5 1.5 %collective-permute-done.1.low_ref = bf16[64,256]{1,0:T(8,128)(2,1)S(1)} collective-permute-done((bf16[64,256]{1,0:T(8,128)(2,1)S(1)}, bf16[64,256]{1,0:T(8,128)(2,1)S(1)}, u32[]{:S(2)}, u32[]{:S(2)}) %collective-permute-start.1) | collective-permute-done | bytes 32800 | tf_op jit(solution)/shard_map/ppermute | solution.py:251
  15.0 1.2 %shard_map.69 = (f32[16,9,16,128]{3,2,1,0:T(8,128)S(1)}, bf16[16,9,16,128]{3,2,1,0:T(8,128)(2,1)S(1)}) custom-call(bf16[64,256]{1,0:T(8,128)(2,1)S(1)} %collective-permute-done.1.low_ref, bf16[4,768,256]{2,1,0:T(8,128)(2,1)S(1)} %get-tuple-element.15.per_ref, bf16[2,256,768]{2,1,0:T(8,128)(2,1)S(1)} %get-tuple-element.16.turn_ref, ...), custom_call_target="tpu_custom_call" | custom-call | tf_op jit(solution)/shard_map/pallas_call | solution.py:259
  16.3 1.9 %collective-permute-start.3 = (bf16[16,9,16,128]{3,2,1,0:T(8,128)(2,1)S(1)}, bf16[16,9,16,128]{3,2,1,0:T(8,128)(2,1)S(1)}, u32[]{:S(2)}, u32[]{:S(2)}) collective-permute-start(bf16[16,9,16,128]{3,2,1,0:T(8,128)(2,1)S(1)} %get-tuple-element.19), channel_id=1, source_target_pairs={{0,1},{1,0},{2,3},{3,2},{4,5},{5,4},{6,7},{7,6},{8,9},{9,8},{10,11... | collective-permute-start | bytes 1769480 | tf_op jit(solution)/shard_map/ppermute | solution.py:262
  18.2 0.0 copy-done.4
  18.2 0.1 constant_dynamic-slice_fusion
  18.4 9.6 %all_to_all.20 = bf16[4,16,1152]{2,1,0:T(8,128)(2,1)S(1)} all-to-all(bf16[4,16,1152]{2,1,0:T(8,128)(2,1)S(1)} %broadcast_in_dim.21), channel_id=1, replica_groups=mesh['x'=4,'zl'=4,'y'=8,'zh'=2,'core'=2] {'zl'}, dimensions={0} | all-to-all | bytes 294912 | tf_op jit(solution)/shard_map/all_to_all | solution.py:235
  28.0 0.9 broadcast_in_dim.23
  28.8 4.0 %all-to-all-start.1 = ((bf16[4,64,1152]{2,1,0:T(8,128)(2,1)}), bf16[4,64,1152]{2,1,0:T(8,128)(2,1)S(1)}, u32[]{:S(2)}, u32[]{:S(2)}) async-start(bf16[4,64,1152]{2,1,0:T(8,128)(2,1)} %broadcast_in_dim.23), calls=%async_computation.1 | async-start | bytes 1179648 | tf_op jit(solution)/shard_map/all_to_all | solution.py:235
  32.8 0.0 collective-permute-done.3
  32.8 0.9 %add_convert_fusion = bf16[16,9,16,128]{3,2,1,0:T(8,128)(2,1)} fusion(f32[16,9,16,128]{3,2,1,0:T(8,128)S(1)} %get-tuple-element.18, bf16[16,9,16,128]{3,2,1,0:T(8,128)(2,1)S(1)} %collective-permute-done.3), kind=kLoop, calls=%fused_computation | loop fusion | flops 884736 | bytes 2359296 | tf_op jit(solution)/shard_map/convert_element_type | solution.py:263
  33.8 6.8 %all-to-all-done.1 = bf16[4,64,1152]{2,1,0:T(8,128)(2,1)S(1)} async-done(((bf16[4,64,1152]{2,1,0:T(8,128)(2,1)}), bf16[4,64,1152]{2,1,0:T(8,128)(2,1)S(1)}, u32[]{:S(2)}, u32[]{:S(2)}) %all-to-all-start.1) | async-done | bytes 589856 | tf_op jit(solution)/shard_map/all_to_all | solution.py:235
  40.6 3.6 %all-to-all-start.2 = ((bf16[4,576,128]{2,1,0:T(8,128)(2,1)}), bf16[4,576,128]{2,1,0:T(8,128)(2,1)S(1)}, u32[]{:S(2)}, u32[]{:S(2)}) async-start(bf16[4,576,128]{2,1,0:T(8,128)(2,1)} %bitcast.35), calls=%async_computation.2 | async-start | bytes 1179648 | tf_op jit(solution)/shard_map/all_to_all | solution.py:264
  44.2 5.3 %collective-permute-start = (bf16[256,1152]{1,0:T(8,128)(2,1)S(1)}, bf16[256,1152]{1,0:T(8,128)(2,1)}, u32[]{:S(2)}, u32[]{:S(2)}) collective-permute-start(bf16[256,1152]{1,0:T(8,128)(2,1)S(1)} %bitcast.31), channel_id=1, source_target_pairs={{0,1},{1,0},{2,3},{3,2},{4,5},{5,4},{6,7},{7,6},{8,9},{9,8},{10,11... | collective-permute-start | bytes 1769480 | tf_op jit(solution)/shard_map/ppermute | solution.py:268
  49.5 2.0 %all-to-all-done.2.parts_ref = bf16[4,576,128]{2,1,0:T(8,128)(2,1)S(1)} async-done(((bf16[4,576,128]{2,1,0:T(8,128)(2,1)}), bf16[4,576,128]{2,1,0:T(8,128)(2,1)S(1)}, u32[]{:S(2)}, u32[]{:S(2)}) %all-to-all-start.2) | async-done | bytes 589856 | tf_op jit(solution)/shard_map/all_to_all | solution.py:264
  51.5 0.9 %shard_map.70 = bf16[16,4,8,144]{3,2,1,0:T(8,128)(2,1)} custom-call(bf16[4,576,128]{2,1,0:T(8,128)(2,1)S(1)} %all-to-all-done.2.parts_ref), custom_call_target="tpu_custom_call" | custom-call | tf_op jit(solution)/shard_map/pallas_call | solution.py:265
  52.4 13.8 %all-to-all-start.3 = ((bf16[64,8,144]{2,1,0:T(8,128)(2,1)}), bf16[64,8,144]{2,1,0:T(8,128)(2,1)S(1)}, u32[]{:S(2)}, u32[]{:S(2)}) async-start(bf16[64,8,144]{2,1,0:T(8,128)(2,1)} %bitcast.13), calls=%async_computation.3 | async-start | bytes 524288 | tf_op jit(solution)/shard_map/all_to_all | solution.py:266
  66.2 11.5 %collective-permute-start.2 = (bf16[128,256]{1,0:T(8,128)(2,1)S(1)}, bf16[128,256]{1,0:T(8,128)(2,1)S(1)}, u32[]{:S(2)}, u32[]{:S(2)}) collective-permute-start(bf16[128,256]{1,0:T(8,128)(2,1)S(1)} %slice_bitcast_fusion), channel_id=1, source_target_pairs={{0,1},{1,2},{2,3},{3,4},{4,5},{5,6},{6,7},{7,8},{8,9},{9,10},{10,1... | collective-permute-start | bytes 196616 | tf_op jit(solution)/shard_map/ppermute | solution.py:267
  77.8 0.1 pad_add_fusion.place_ref
  77.9 0.0 collective-permute-done.other_ref
  77.9 5.4 %shard_map.66 = (bf16[24,128,256]{2,1,0:T(8,128)(2,1)}, bf16[256,2304]{1,0:T(8,128)(2,1)S(1)}, f32[8,144]{1,0:T(8,128)S(1)}, f32[1,16]{1,0:T(1,128)}) custom-call(s32[4]{0:T(128)S(1)} %pad_add_fusion.place_ref, bf16[256,1152]{1,0:T(8,128)(2,1)S(1)} %bitcast.32, bf16[256,1152]{1,0:T(8,128)(2,1)} %collective-permute-done.other_ref, ...), custom_call_target="tpu_custom_call" | custom-call | tf_op jit(solution)/shard_map/pallas_call | solution.py:270
  83.3 0.0 collective-permute-done.2.up_ref
  83.3 2.3 %shard_map.67 = bf16[12,64,256]{2,1,0:T(8,128)(2,1)} custom-call(bf16[256,2304]{1,0:T(8,128)(2,1)S(1)} %get-tuple-element.13.w_ref, bf16[128,256]{1,0:T(8,128)(2,1)S(1)} %collective-permute-done.2.up_ref, bf16[24,128,256]{2,1,0:T(8,128)(2,1)S(1)} %bitcast.30), custom_call_target="tpu_custom_call" | custom-call | tf_op jit(solution)/shard_map/pallas_call | solution.py:277
  85.6 0.0 all-to-all-done.3
  85.6 0.1 convert_reduce_fusion
  85.7 0.1 reshape.41
  85.7 0.6 copy.11
  (12 shorter events, 0.1 us)
Async XLA Ops:
  1.4 13.6 %collective-permute-start.1 = (bf16[64,256]{1,0:T(8,128)(2,1)S(1)}, bf16[64,256]{1,0:T(8,128)(2,1)S(1)}, u32[]{:S(2)}, u32[]{:S(2)}) collective-permute-start(bf16[64,256]{1,0:T(8,128)(2,1)S(1)} %slice_bitcast_fusion.1), channel_id=1, source_target_pairs={{1,0},{2,1},{3,2},{4,3},{5,4},{6,5},{7,6},{8,7},{9,8},{10,9},{11,1... | collective-permute-start | bytes 98312 | tf_op jit(solution)/shard_map/ppermute | solution.py:251
  10.1 1.4 %copy-start = (bf16[1,24,128,256]{3,2,1,0:T(8,128)(2,1)S(1)}, bf16[1,24,128,256]{3,2,1,0:T(8,128)(2,1)}, u32[]{:S(2)}) copy-start(bf16[1,24,128,256]{3,2,1,0:T(8,128)(2,1)} %param.3) | copy-start | bytes 4718596
  11.6 1.0 %copy-start.2 = (bf16[1,12,64,256]{3,2,1,0:T(8,128)(2,1)S(1)}, bf16[1,12,64,256]{3,2,1,0:T(8,128)(2,1)}, u32[]{:S(2)}) copy-start(bf16[1,12,64,256]{3,2,1,0:T(8,128)(2,1)} %param.5) | copy-start | bytes 1179652
  15.0 3.2 %copy-start.4 = (bf16[16,3,3,256]{3,0,2,1:T(8,128)(2,1)S(1)}, bf16[16,3,3,256]{3,0,2,1:T(8,128)(2,1)}, u32[]{:S(2)}) copy-start(bf16[16,3,3,256]{3,0,2,1:T(8,128)(2,1)} %param.4) | copy-start | bytes 221188
  16.3 16.6 %collective-permute-start.3 = (bf16[16,9,16,128]{3,2,1,0:T(8,128)(2,1)S(1)}, bf16[16,9,16,128]{3,2,1,0:T(8,128)(2,1)S(1)}, u32[]{:S(2)}, u32[]{:S(2)}) collective-permute-start(bf16[16,9,16,128]{3,2,1,0:T(8,128)(2,1)S(1)} %get-tuple-element.19), channel_id=1, source_target_pairs={{0,1},{1,0},{2,3},{3,2},{4,5},{5,4},{6,7},{7,6},{8,9},{9,8},{10,11... | collective-permute-start | bytes 1769480 | tf_op jit(solution)/shard_map/ppermute | solution.py:262
  28.8 11.8 %all-to-all-start.1 = ((bf16[4,64,1152]{2,1,0:T(8,128)(2,1)}), bf16[4,64,1152]{2,1,0:T(8,128)(2,1)S(1)}, u32[]{:S(2)}, u32[]{:S(2)}) async-start(bf16[4,64,1152]{2,1,0:T(8,128)(2,1)} %broadcast_in_dim.23), calls=%async_computation.1 | async-start | bytes 1179648 | tf_op jit(solution)/shard_map/all_to_all | solution.py:235
  40.6 25.6 %copy-start.1 = (bf16[1,24,128,256]{3,2,1,0:T(8,128)(2,1)S(1)}, bf16[1,24,128,256]{3,2,1,0:T(8,128)(2,1)}, u32[]{:S(2)}) copy-start(bf16[1,24,128,256]{3,2,1,0:T(8,128)(2,1)} %param.3) | copy-start | bytes 4718596
  40.6 37.3 %copy-start.3 = (bf16[1,12,64,256]{3,2,1,0:T(8,128)(2,1)S(1)}, bf16[1,12,64,256]{3,2,1,0:T(8,128)(2,1)}, u32[]{:S(2)}) copy-start(bf16[1,12,64,256]{3,2,1,0:T(8,128)(2,1)} %param.5) | copy-start | bytes 1179652
  40.6 10.9 %all-to-all-start.2 = ((bf16[4,576,128]{2,1,0:T(8,128)(2,1)}), bf16[4,576,128]{2,1,0:T(8,128)(2,1)S(1)}, u32[]{:S(2)}, u32[]{:S(2)}) async-start(bf16[4,576,128]{2,1,0:T(8,128)(2,1)} %bitcast.35), calls=%async_computation.2 | async-start | bytes 1179648 | tf_op jit(solution)/shard_map/all_to_all | solution.py:264
  44.2 33.6 %collective-permute-start = (bf16[256,1152]{1,0:T(8,128)(2,1)S(1)}, bf16[256,1152]{1,0:T(8,128)(2,1)}, u32[]{:S(2)}, u32[]{:S(2)}) collective-permute-start(bf16[256,1152]{1,0:T(8,128)(2,1)S(1)} %bitcast.31), channel_id=1, source_target_pairs={{0,1},{1,0},{2,3},{3,2},{4,5},{5,4},{6,7},{7,6},{8,9},{9,8},{10,11... | collective-permute-start | bytes 1769480 | tf_op jit(solution)/shard_map/ppermute | solution.py:268
  52.4 33.2 %all-to-all-start.3 = ((bf16[64,8,144]{2,1,0:T(8,128)(2,1)}), bf16[64,8,144]{2,1,0:T(8,128)(2,1)S(1)}, u32[]{:S(2)}, u32[]{:S(2)}) async-start(bf16[64,8,144]{2,1,0:T(8,128)(2,1)} %bitcast.13), calls=%async_computation.3 | async-start | bytes 524288 | tf_op jit(solution)/shard_map/all_to_all | solution.py:266
  66.2 17.1 %collective-permute-start.2 = (bf16[128,256]{1,0:T(8,128)(2,1)S(1)}, bf16[128,256]{1,0:T(8,128)(2,1)S(1)}, u32[]{:S(2)}, u32[]{:S(2)}) collective-permute-start(bf16[128,256]{1,0:T(8,128)(2,1)S(1)} %slice_bitcast_fusion), channel_id=1, source_target_pairs={{0,1},{1,2},{2,3},{3,4},{4,5},{5,6},{6,7},{7,8},{8,9},{9,10},{10,1... | collective-permute-start | bytes 196616 | tf_op jit(solution)/shard_map/ppermute | solution.py:267

commit v3 on v2

--- a/solution.py
+++ b/solution.py
@@ -98,10 +98,11 @@
     half = CH // 2
 
     def halves(lower_ref, upper_ref):
-        for t in range(9):
-            lanes = slice(t * half, (t + 1) * half)
-            w_ref[:, t * CH : t * CH + half] = lower_ref[:, lanes]
-            w_ref[:, t * CH + half : (t + 1) * CH] = upper_ref[:, lanes]
+        for f in range(16):
+            rows = slice(f * 16, (f + 1) * 16)
+            for t in range(9):
+                w_ref[rows, t * CH : t * CH + half] = lower_ref[f, t]
+                w_ref[rows, t * CH + half : (t + 1) * CH] = upper_ref[f, t]
 
     @pl.when(core == 0)
     def _():
@@ -214,7 +215,28 @@
         total = total + parts_ref[k].astype(F32)
     turned = total.T
     for k in range(4):
-        out_ref[:, k] = turned[:, 144 * k : 144 * (k + 1)].reshape(16, 8, 144).astype(BF)
+        block = turned[:, 144 * k : 144 * (k + 1)].reshape(16, 8, 144)
+        out_ref[:, k, :, :144] = block[:, :4].astype(BF)
+        out_ref[:, k, :, 144:] = block[:, 4:].astype(BF)
+
+
+def panel_kernel(core_ref, kernel_ref, out_ref):
+    @pl.when(core_ref[0] == 0)
+    def _():
+        for k in range(4):
+            out_ref[k] = kernel_ref[:, :, : CH // 2]
+
+    @pl.when(core_ref[0] == 1)
+    def _():
+        for k in range(4):
+            out_ref[k] = kernel_ref[:, :, CH // 2 :]
+
+
+def final_kernel(parts_ref, pen_ref, out_ref):
+    both = jnp.sum(parts_ref[...].astype(F32), axis=0)
+    total = jnp.concatenate([both[:, :144], both[:, 144:]], axis=0) / (R * 32) + (4.0 * PEN_WEIGHT) * pen_ref[...]
+    for t in range(9):
+        out_ref[t] = total[:, 16 * t : 16 * (t + 1)]
 
 
 def call(kernel, out_shape, scratch=(), n_scalar=0, n_in=0):
@@ -245,9 +267,12 @@
     space = lax.axis_index(("y", "zh", "core"))
     n_space = 32
     swap = [(0, 1), (1, 0)]
-    panel = lax.dynamic_index_in_dim(kernel.reshape(16, 9, 2, CH // 2), core, 2, keepdims=False)
-    own = spread(panel.reshape(16, 9 * CH // 2), "zl", 4).reshape(64, 9 * CH // 2)
-    mine = spread(own, "x", 4).reshape(256, 9 * CH // 2)
+    panel = jnp.transpose(kernel, (1, 2, 0, 3)).reshape(9, 16, CH)
+    panels = call(panel_kernel, S((4, 9, 16, CH // 2), BF), n_scalar=1, n_in=1)(
+        core.astype(jnp.int32).reshape(1), panel
+    )
+    own = lax.all_to_all(panels, "zl", 0, 0, tiled=True)
+    mine = spread(own, "x", 4).reshape(16, 9, 16, CH // 2)
     low = lax.ppermute(cotangent[0], ("y", "zh", "core"), [(i + 1, i) for i in range(n_space - 1)])
     per, turn, turn_low = call(
         prep_kernel,
@@ -262,8 +287,8 @@
     recv = lax.ppermute(send, "core", swap)
     both = (keep + recv.astype(F32)).astype(BF).reshape(4, 576, 128)
     parts = lax.all_to_all(both, "x", 0, 0, tiled=True)
-    turned = call(sum_kernel, S((16, 4, 8, 144), BF), n_in=1)(parts)
-    pieces = lax.all_to_all(turned.reshape(64, 8, 144), ("y", "zh", "zl"), 0, 0, tiled=True)
+    turned = call(sum_kernel, S((16, 4, 4, 288), BF), n_in=1)(parts)
+    pieces = lax.all_to_all(turned.reshape(64, 4, 288), ("y", "zh", "zl"), 0, 0, tiled=True)
     up = lax.ppermute(images[ROWS - 1], ("y", "zh", "core"), [(i, i + 1) for i in range(n_space - 1)])
     other = lax.ppermute(mine, "core", swap)
     place = jnp.stack([core, x, zl, space]).astype(jnp.int32)
@@ -280,8 +305,8 @@
         scratch=[pltpu.VMEM((POS, CH), BF)] * 4 + [pltpu.VMEM((POS, CH), F32)] * 2,
         n_in=3,
     )(whole, up, images)
-    own = jnp.sum(pieces.astype(F32), axis=0) / (R * n_space) + (4.0 * PEN_WEIGHT) * pen
-    grad_kernel = jnp.transpose(own.reshape(8, 9, 16), (2, 1, 0)).reshape(16, 3, 3, 8)
+    grads = call(final_kernel, S((9, 8, 16), F32), n_in=2)(pieces, pen)
+    grad_kernel = jnp.transpose(grads.reshape(3, 3, 8, 16), (3, 0, 1, 2))
     return output[None], grad_input[None], grad_kernel, rows.reshape(16)
 
 

time: 87 us -> 86.9 us (level)
  Pallas kernels: 10.8 us -> 11.8 us
    pallas_call x1 -> x3, Pallas kernels: 0.94 us -> 1.85 us  [the longest x1 0.97 us: body(): turned = call(sum_kernel, S((16, 4, 4, 288), BF), n_in=1)(parts)]
    unnamed x12 -> x10, local copies, waits for them, and re-layouts: 2.45 us -> 2.41 us
where the time goes in v3:
time: 86.9 us; the launch traced here: 86.3 us
  starting transfers between devices  48.9 us (56%)
  Pallas kernels  11.8 us (14%)
  waiting for transfers between devices  10.3 us (12%)
  blocking collectives  9.57 us (11%)
  local copies, waits for them, and re-layouts  4.07 us (5%)
  other arithmetic  1.02 us (1%)
    all_to_all x1, starting transfers between devices, body(): lax.all_to_all(turned.reshape(64, 4, 288), ('y', 'zh', 'zl'), 0, 0, tiled...  13.8 us
    ppermute x1, starting transfers between devices, body(): lax.ppermute(images[ROWS - 1], ('y', 'zh', 'core'), [(i, i + 1) for i in...  11.5 us
    all_to_all x1, blocking collectives, body(): own = lax.all_to_all(panels, 'zl', 0, 0, tiled=True)  9.57 us
    ppermute x1, starting transfers between devices, body(): lax.ppermute(cotangent[0], ('y', 'zh', 'core'), [(i + 1, i) for i in rang...  8.73 us
    all_to_all x1, waiting for transfers between devices, spread(): lax.all_to_all(jnp.broadcast_to(block[None], (size,) + block.shape), axis...  6.83 us
    pallas_call x1, Pallas kernels, body(): call(back_kernel, (S((ROWS, COLS, CH), BF), S((CH, 9 * CH), BF), S((8, 14...  5.43 us
    ppermute x1, starting transfers between devices, body(): other = lax.ppermute(mine, 'core', swap)  5.27 us
    all_to_all x1, starting transfers between devices, spread(): lax.all_to_all(jnp.broadcast_to(block[None], (size,) + block.shape), axis...  4.01 us
  transfers between devices with their start and end apart: 7, of which 3 were waited for; matrix products, arithmetic and copies ran while one was open for 2% of the time, Pallas kernels for 11%

profile of v3, /device:TPU:1, one launch (start us, length us, event | category | flops | bytes accessed | tf_op | source)
XLA Modules:
  0.0 86.3 jit_solution(4115822217551641194)
XLA Ops:
  0.6 0.8 slice_bitcast_fusion.1
  1.4 8.7 %collective-permute-start.1 = (bf16[64,256]{1,0:T(8,128)(2,1)S(1)}, bf16[64,256]{1,0:T(8,128)(2,1)S(1)}, u32[]{:S(2)}, u32[]{:S(2)}) collective-permute-start(bf16[64,256]{1,0:T(8,128)(2,1)S(1)} %slice_bitcast_fusion.1), channel_id=1, source_target_pairs={{1,0},{2,1},{3,2},{4,3},{5,4},{6,5},{7,6},{8,7},{9,8},{10,9},{11,1... | collective-permute-start | bytes 98312 | tf_op jit(solution)/shard_map/ppermute | solution.py:276
  10.1 0.0 copy-start
  10.2 1.4 %copy-done = bf16[1,24,128,256]{3,2,1,0:T(8,128)(2,1)S(1)} copy-done((bf16[1,24,128,256]{3,2,1,0:T(8,128)(2,1)S(1)}, bf16[1,24,128,256]{3,2,1,0:T(8,128)(2,1)}, u32[]{:S(2)}) %copy-start) | copy-done | bytes 1572888
  11.6 0.0 copy-start.2
  11.6 1.0 %copy-done.2 = bf16[1,12,64,256]{3,2,1,0:T(8,128)(2,1)S(1)} copy-done((bf16[1,12,64,256]{3,2,1,0:T(8,128)(2,1)S(1)}, bf16[1,12,64,256]{3,2,1,0:T(8,128)(2,1)}, u32[]{:S(2)}) %copy-start.2) | copy-done | bytes 393240
  12.5 1.0 %shard_map.69 = (bf16[4,768,256]{2,1,0:T(8,128)(2,1)S(1)}, bf16[2,256,768]{2,1,0:T(8,128)(2,1)S(1)}, bf16[2,256,704]{2,1,0:T(8,128)(2,1)S(1)}) custom-call(s32[1]{0:T(128)} %bitcast.core_ref, bf16[24,128,256]{2,1,0:T(8,128)(2,1)S(1)} %bitcast.22, bf16[12,64,256]{2,1,0:T(8,128)(2,1)S(1)} %bitcast.26), custom_call_target="tpu_custom_call" | custom-call | tf_op jit(solution)/shard_map/pallas_call | solution.py:277
  13.5 1.5 %collective-permute-done.1.low_ref = bf16[64,256]{1,0:T(8,128)(2,1)S(1)} collective-permute-done((bf16[64,256]{1,0:T(8,128)(2,1)S(1)}, bf16[64,256]{1,0:T(8,128)(2,1)S(1)}, u32[]{:S(2)}, u32[]{:S(2)}) %collective-permute-start.1) | collective-permute-done | bytes 32800 | tf_op jit(solution)/shard_map/ppermute | solution.py:276
  15.0 1.2 %shard_map.70 = (f32[16,9,16,128]{3,2,1,0:T(8,128)S(1)}, bf16[16,9,16,128]{3,2,1,0:T(8,128)(2,1)S(1)}) custom-call(bf16[64,256]{1,0:T(8,128)(2,1)S(1)} %collective-permute-done.1.low_ref, bf16[4,768,256]{2,1,0:T(8,128)(2,1)S(1)} %get-tuple-element.15.per_ref, bf16[2,256,768]{2,1,0:T(8,128)(2,1)S(1)} %get-tuple-element.16.turn_ref, ...), custom_call_target="tpu_custom_call" | custom-call | tf_op jit(solution)/shard_map/pallas_call | solution.py:284
  16.3 1.9 %collective-permute-start.3 = (bf16[16,9,16,128]{3,2,1,0:T(8,128)(2,1)S(1)}, bf16[16,9,16,128]{3,2,1,0:T(8,128)(2,1)S(1)}, u32[]{:S(2)}, u32[]{:S(2)}) collective-permute-start(bf16[16,9,16,128]{3,2,1,0:T(8,128)(2,1)S(1)} %get-tuple-element.19), channel_id=1, source_target_pairs={{0,1},{1,0},{2,3},{3,2},{4,5},{5,4},{6,7},{7,6},{8,9},{9,8},{10,11... | collective-permute-start | bytes 1769480 | tf_op jit(solution)/shard_map/ppermute | solution.py:287
  18.2 0.0 copy-done.4
  18.2 9.6 %all_to_all.20 = bf16[4,9,16,128]{3,2,1,0:T(8,128)(2,1)S(1)} all-to-all(bf16[4,9,16,128]{3,2,1,0:T(8,128)(2,1)S(1)} %shard_map.66), channel_id=1, replica_groups=mesh['x'=4,'zl'=4,'y'=8,'zh'=2,'core'=2] {'zl'}, dimensions={0} | all-to-all | bytes 294912 | tf_op jit(solution)/shard_map/all_to_all | solution.py:274
  27.8 0.9 %broadcast_in_dim.12 = bf16[4,4,9,16,128]{4,3,2,1,0:T(8,128)(2,1)} broadcast(bf16[4,9,16,128]{3,2,1,0:T(8,128)(2,1)S(1)} %all_to_all.20), dimensions={1,2,3,4} | broadcast | bytes 737280 | tf_op jit(solution)/shard_map/broadcast_in_dim | solution.py:257
  28.7 4.0 %all-to-all-start.1 = ((bf16[4,4,9,16,128]{4,3,2,1,0:T(8,128)(2,1)}), bf16[4,4,9,16,128]{4,3,2,1,0:T(8,128)(2,1)S(1)}, u32[]{:S(2)}, u32[]{:S(2)}) async-start(bf16[4,4,9,16,128]{4,3,2,1,0:T(8,128)(2,1)} %broadcast_in_dim.12), calls=%async_computation.1 | async-start | bytes 1179648 | tf_op jit(solution)/shard_map/all_to_all | solution.py:257
  32.7 0.0 collective-permute-done.3
  32.7 0.9 %add_convert_fusion = bf16[16,9,16,128]{3,2,1,0:T(8,128)(2,1)} fusion(f32[16,9,16,128]{3,2,1,0:T(8,128)S(1)} %get-tuple-element.18, bf16[16,9,16,128]{3,2,1,0:T(8,128)(2,1)S(1)} %collective-permute-done.3), kind=kLoop, calls=%fused_computation | loop fusion | flops 884736 | bytes 2359296 | tf_op jit(solution)/shard_map/convert_element_type | solution.py:288
  33.6 6.8 %all-to-all-done.1 = bf16[4,4,9,16,128]{4,3,2,1,0:T(8,128)(2,1)S(1)} async-done(((bf16[4,4,9,16,128]{4,3,2,1,0:T(8,128)(2,1)}), bf16[4,4,9,16,128]{4,3,2,1,0:T(8,128)(2,1)S(1)}, u32[]{:S(2)}, u32[]{:S(2)}) %all-to-all-start.1) | async-done | bytes 589856 | tf_op jit(solution)/shard_map/all_to_all | solution.py:257
  40.5 3.6 %all-to-all-start.2 = ((bf16[4,576,128]{2,1,0:T(8,128)(2,1)}), bf16[4,576,128]{2,1,0:T(8,128)(2,1)S(1)}, u32[]{:S(2)}, u32[]{:S(2)}) async-start(bf16[4,576,128]{2,1,0:T(8,128)(2,1)} %bitcast.29), calls=%async_computation.2 | async-start | bytes 1179648 | tf_op jit(solution)/shard_map/all_to_all | solution.py:289
  44.1 5.3 %collective-permute-start = (bf16[16,9,16,128]{3,2,1,0:T(8,128)(2,1)S(1)}, bf16[16,9,16,128]{3,2,1,0:T(8,128)(2,1)}, u32[]{:S(2)}, u32[]{:S(2)}) collective-permute-start(bf16[16,9,16,128]{3,2,1,0:T(8,128)(2,1)S(1)} %bitcast.24), channel_id=1, source_target_pairs={{0,1},{1,0},{2,3},{3,2},{4,5},{5,4},{6,7},{7,6},{8,9},{9,8},{10,11... | collective-permute-start | bytes 1769480 | tf_op jit(solution)/shard_map/ppermute | solution.py:293
  49.4 2.0 %all-to-all-done.2.parts_ref = bf16[4,576,128]{2,1,0:T(8,128)(2,1)S(1)} async-done(((bf16[4,576,128]{2,1,0:T(8,128)(2,1)}), bf16[4,576,128]{2,1,0:T(8,128)(2,1)S(1)}, u32[]{:S(2)}, u32[]{:S(2)}) %all-to-all-start.2) | async-done | bytes 589856 | tf_op jit(solution)/shard_map/all_to_all | solution.py:289
  51.3 1.0 %shard_map.71 = bf16[16,4,4,288]{3,2,1,0:T(4,128)(2,1)} custom-call(bf16[4,576,128]{2,1,0:T(8,128)(2,1)S(1)} %all-to-all-done.2.parts_ref), custom_call_target="tpu_custom_call" | custom-call | tf_op jit(solution)/shard_map/pallas_call | solution.py:290
  52.3 13.8 %all-to-all-start.3 = ((bf16[64,4,288]{2,1,0:T(4,128)(2,1)}), bf16[64,4,288]{2,1,0:T(4,128)(2,1)S(1)}, u32[]{:S(2)}, u32[]{:S(2)}) async-start(bf16[64,4,288]{2,1,0:T(4,128)(2,1)} %bitcast.14), calls=%async_computation.3 | async-start | bytes 393216 | tf_op jit(solution)/shard_map/all_to_all | solution.py:291
  66.1 0.0 copy-done.1
  66.1 11.5 %collective-permute-start.2 = (bf16[128,256]{1,0:T(8,128)(2,1)S(1)}, bf16[128,256]{1,0:T(8,128)(2,1)S(1)}, u32[]{:S(2)}, u32[]{:S(2)}) collective-permute-start(bf16[128,256]{1,0:T(8,128)(2,1)S(1)} %slice_bitcast_fusion), channel_id=1, source_target_pairs={{0,1},{1,2},{2,3},{3,4},{4,5},{5,6},{6,7},{7,8},{8,9},{9,10},{10,1... | collective-permute-start | bytes 196616 | tf_op jit(solution)/shard_map/ppermute | solution.py:292
  77.7 0.1 pad_add_fusion.place_ref
  77.8 0.0 collective-permute-done.other_ref
  77.8 0.0 copy-done.3
  77.8 5.4 %shard_map.67 = (bf16[24,128,256]{2,1,0:T(8,128)(2,1)}, bf16[256,2304]{1,0:T(8,128)(2,1)S(1)}, f32[8,144]{1,0:T(8,128)S(1)}, f32[1,16]{1,0:T(1,128)}) custom-call(s32[4]{0:T(128)S(1)} %pad_add_fusion.place_ref, bf16[16,9,16,128]{3,2,1,0:T(8,128)(2,1)S(1)} %bitcast.25, bf16[16,9,16,128]{3,2,1,0:T(8,128)(2,1)} %collective-permute-done.other_ref, ...), custom_call_target="tpu_custom_call" | custom-call | tf_op jit(solution)/shard_map/pallas_call | solution.py:295
  83.2 0.0 collective-permute-done.2.up_ref
  83.2 2.3 %shard_map.68 = bf16[12,64,256]{2,1,0:T(8,128)(2,1)} custom-call(bf16[256,2304]{1,0:T(8,128)(2,1)S(1)} %get-tuple-element.13.w_ref, bf16[128,256]{1,0:T(8,128)(2,1)S(1)} %collective-permute-done.2.up_ref, bf16[24,128,256]{2,1,0:T(8,128)(2,1)S(1)} %bitcast.23), custom_call_target="tpu_custom_call" | custom-call | tf_op jit(solution)/shard_map/pallas_call | solution.py:302
  85.5 0.0 all-to-all-done.3.parts_ref
  85.5 0.8 shard_map.72
  (5 shorter events, 0.0 us)
Async XLA Ops:
  1.4 13.6 %collective-permute-start.1 = (bf16[64,256]{1,0:T(8,128)(2,1)S(1)}, bf16[64,256]{1,0:T(8,128)(2,1)S(1)}, u32[]{:S(2)}, u32[]{:S(2)}) collective-permute-start(bf16[64,256]{1,0:T(8,128)(2,1)S(1)} %slice_bitcast_fusion.1), channel_id=1, source_target_pairs={{1,0},{2,1},{3,2},{4,3},{5,4},{6,5},{7,6},{8,7},{9,8},{10,9},{11,1... | collective-permute-start | bytes 98312 | tf_op jit(solution)/shard_map/ppermute | solution.py:276
  10.1 1.4 %copy-start = (bf16[1,24,128,256]{3,2,1,0:T(8,128)(2,1)S(1)}, bf16[1,24,128,256]{3,2,1,0:T(8,128)(2,1)}, u32[]{:S(2)}) copy-start(bf16[1,24,128,256]{3,2,1,0:T(8,128)(2,1)} %param.3) | copy-start | bytes 4718596
  11.6 1.0 %copy-start.2 = (bf16[1,12,64,256]{3,2,1,0:T(8,128)(2,1)S(1)}, bf16[1,12,64,256]{3,2,1,0:T(8,128)(2,1)}, u32[]{:S(2)}) copy-start(bf16[1,12,64,256]{3,2,1,0:T(8,128)(2,1)} %param.5) | copy-start | bytes 1179652
  15.0 3.2 %copy-start.4 = (bf16[16,3,3,256]{3,0,2,1:T(8,128)(2,1)S(1)}, bf16[16,3,3,256]{3,0,2,1:T(8,128)(2,1)}, u32[]{:S(2)}) copy-start(bf16[16,3,3,256]{3,0,2,1:T(8,128)(2,1)} %param.4) | copy-start | bytes 221188
  16.3 16.5 %collective-permute-start.3 = (bf16[16,9,16,128]{3,2,1,0:T(8,128)(2,1)S(1)}, bf16[16,9,16,128]{3,2,1,0:T(8,128)(2,1)S(1)}, u32[]{:S(2)}, u32[]{:S(2)}) collective-permute-start(bf16[16,9,16,128]{3,2,1,0:T(8,128)(2,1)S(1)} %get-tuple-element.19), channel_id=1, source_target_pairs={{0,1},{1,0},{2,3},{3,2},{4,5},{5,4},{6,7},{7,6},{8,9},{9,8},{10,11... | collective-permute-start | bytes 1769480 | tf_op jit(solution)/shard_map/ppermute | solution.py:287
  28.7 11.8 %all-to-all-start.1 = ((bf16[4,4,9,16,128]{4,3,2,1,0:T(8,128)(2,1)}), bf16[4,4,9,16,128]{4,3,2,1,0:T(8,128)(2,1)S(1)}, u32[]{:S(2)}, u32[]{:S(2)}) async-start(bf16[4,4,9,16,128]{4,3,2,1,0:T(8,128)(2,1)} %broadcast_in_dim.12), calls=%async_computation.1 | async-start | bytes 1179648 | tf_op jit(solution)/shard_map/all_to_all | solution.py:257
  40.5 25.6 %copy-start.1 = (bf16[1,24,128,256]{3,2,1,0:T(8,128)(2,1)S(1)}, bf16[1,24,128,256]{3,2,1,0:T(8,128)(2,1)}, u32[]{:S(2)}) copy-start(bf16[1,24,128,256]{3,2,1,0:T(8,128)(2,1)} %param.3) | copy-start | bytes 4718596
  40.5 37.3 %copy-start.3 = (bf16[1,12,64,256]{3,2,1,0:T(8,128)(2,1)S(1)}, bf16[1,12,64,256]{3,2,1,0:T(8,128)(2,1)}, u32[]{:S(2)}) copy-start(bf16[1,12,64,256]{3,2,1,0:T(8,128)(2,1)} %param.5) | copy-start | bytes 1179652
  40.5 10.9 %all-to-all-start.2 = ((bf16[4,576,128]{2,1,0:T(8,128)(2,1)}), bf16[4,576,128]{2,1,0:T(8,128)(2,1)S(1)}, u32[]{:S(2)}, u32[]{:S(2)}) async-start(bf16[4,576,128]{2,1,0:T(8,128)(2,1)} %bitcast.29), calls=%async_computation.2 | async-start | bytes 1179648 | tf_op jit(solution)/shard_map/all_to_all | solution.py:289
  44.1 33.7 %collective-permute-start = (bf16[16,9,16,128]{3,2,1,0:T(8,128)(2,1)S(1)}, bf16[16,9,16,128]{3,2,1,0:T(8,128)(2,1)}, u32[]{:S(2)}, u32[]{:S(2)}) collective-permute-start(bf16[16,9,16,128]{3,2,1,0:T(8,128)(2,1)S(1)} %bitcast.24), channel_id=1, source_target_pairs={{0,1},{1,0},{2,3},{3,2},{4,5},{5,4},{6,7},{7,6},{8,9},{9,8},{10,11... | collective-permute-start | bytes 1769480 | tf_op jit(solution)/shard_map/ppermute | solution.py:293
  52.3 33.2 %all-to-all-start.3 = ((bf16[64,4,288]{2,1,0:T(4,128)(2,1)}), bf16[64,4,288]{2,1,0:T(4,128)(2,1)S(1)}, u32[]{:S(2)}, u32[]{:S(2)}) async-start(bf16[64,4,288]{2,1,0:T(4,128)(2,1)} %bitcast.14), calls=%async_computation.3 | async-start | bytes 393216 | tf_op jit(solution)/shard_map/all_to_all | solution.py:291
  66.1 17.1 %collective-permute-start.2 = (bf16[128,256]{1,0:T(8,128)(2,1)S(1)}, bf16[128,256]{1,0:T(8,128)(2,1)S(1)}, u32[]{:S(2)}, u32[]{:S(2)}) collective-permute-start(bf16[128,256]{1,0:T(8,128)(2,1)S(1)} %slice_bitcast_fusion), channel_id=1, source_target_pairs={{0,1},{1,2},{2,3},{3,4},{4,5},{5,6},{6,7},{7,8},{8,9},{9,10},{10,1... | collective-permute-start | bytes 196616 | tf_op jit(solution)/shard_map/ppermute | solution.py:292
